TPU v7x, 128 devices: a whole 4x4x4 slice. The times are simulated.
128 devices in a mesh: row: 8 (over z, core), col: 16 (over y, x).
Axes of the slice: x: 4, y: 4, z: 4, core: 2. Of those that a mesh axis runs over, the one named last changes fastest.
Arguments:
- front_entries: float32 [16384, 16384], P(None, ('row', 'col')), as said below
- child_updates: float32 [4096, 128, 128], P(('row', 'col')), may hold values from -1 to 1
- row_maps: int32 [4096, 128], P(('row', 'col')), may hold values from 0 to 127, each once within a row
- col_maps: int32 [4096, 128], P(('row', 'col')), may hold values from 0 to 127, each once within a row
- target_columns: int32 [4096, 1], P(('row', 'col')), may hold values from 0 to 127; in each aligned block of 32 rows (0 to 31, 32 to 63, ...) at most 2 rows name the same one
- row_offsets: int32 [4096, 1], P(('row', 'col')), may hold values from 0 to 127
Outputs:
- factored: float32 [16, 8, 8, 16, 128, 128], P(None, 'row', None, 'col')
Inputs may be any that keep to these rules, and one draw needn't show every extreme that they name: `target_columns`: within the rows of one device (aligned blocks of 32 rows) no block column is named more than 2 times; some device names one block column exactly 2 times. `row_maps`: each row is a permutation of 0 to 127. `col_maps`: each row is a permutation of 0 to 127. `front_entries`: entries off the diagonal lie in [0, 2]; diagonal entries lie between 2.5 and 3.5 times the square root of 16384.
All inputs are finite; a program needn't handle non-finite values.
Results may differ from a plain program's by a relative error of at most 0.0001.
Values sent between devices are 32-bit elements; how exact they have to be, the bound alone decides.
A program may use at most 192 MiB of HBM per device.

v0:
```python
import jax
import jax.numpy as jnp
from jax import lax
from jax.sharding import PartitionSpec as P

SLOTS = 2
PANELS = 2


PRECISE = lax.Precision.HIGHEST


def broadcast(value, axis, source):
    kept = jnp.where(lax.axis_index(axis) == source, value, 0).astype(value.dtype)
    return lax.psum(kept, axis)


def place_tiles(tile_set, row_set, col_set):
    levels = jnp.arange(tile_set.shape[1], dtype=jnp.int32)
    row_onehot = (row_set[:, :, None] == levels).astype(jnp.float32)
    col_onehot = (col_set[:, :, None] == levels).astype(jnp.float32)
    half_done = jnp.einsum("nij,njb->nib", tile_set, col_onehot, precision=PRECISE)
    return jnp.einsum("nia,nib->nab", row_onehot, half_done, precision=PRECISE)


def local(front_entries, child_updates, row_maps, col_maps, target_columns, row_offsets):
    grid_rows = lax.axis_size("row")
    grid_cols = lax.axis_size("col")
    block_count = grid_rows * grid_cols
    tile_edge = child_updates.shape[1]
    held_count = child_updates.shape[0]
    columns = target_columns[:, 0]
    offsets = row_offsets[:, 0]
    target_rows = columns + offsets % (block_count - columns)
    placed = place_tiles(child_updates, row_maps, col_maps)
    serial = jnp.arange(held_count, dtype=jnp.int32)
    earlier = (columns[:, None] == columns[None, :]) & (serial[None, :] < serial[:, None])
    slot_rank = jnp.sum(earlier.astype(jnp.int32), axis=1)
    position = columns * SLOTS + slot_rank
    outgoing = (
        jnp.zeros((block_count * SLOTS, tile_edge, tile_edge), jnp.float32).at[position].set(placed)
    )
    targets = jnp.zeros((block_count * SLOTS,), jnp.int32).at[position].set(target_rows)
    arrived, landing = (
        lax.all_to_all(outgoing, ("row", "col"), split_axis=0, concat_axis=0, tiled=True),
        lax.all_to_all(targets, ("row", "col"), split_axis=0, concat_axis=0, tiled=True),
    )
    own_blocks = front_entries.reshape(block_count, tile_edge, tile_edge)
    column_blocks = own_blocks + jax.ops.segment_sum(arrived, landing, num_segments=block_count)
    grid_tiles = lax.all_to_all(
        column_blocks.reshape(block_count // grid_rows, grid_rows, tile_edge, tile_edge),
        "row",
        split_axis=1,
        concat_axis=1,
        tiled=True,
    )
    my_row = lax.axis_index("row")
    my_col = lax.axis_index("col")
    block_rows = jnp.arange(block_count // grid_rows, dtype=jnp.int32) * grid_rows + my_row
    block_cols = jnp.arange(block_count // grid_cols, dtype=jnp.int32) * grid_cols + my_col
    stride = grid_cols // grid_rows
    for panel_idx in range(PANELS):
        local_row = panel_idx // grid_rows
        prepare_local_col = panel_idx // grid_cols
        pivot_tile = broadcast(
            grid_tiles[local_row, prepare_local_col], "row", panel_idx % grid_rows
        )
        symmetric = jnp.tril(pivot_tile) + jnp.tril(pivot_tile, -1).T
        pivot_factor = jnp.linalg.cholesky(symmetric)
        panel_rows = grid_tiles[:, prepare_local_col].reshape(-1, tile_edge)
        solved = jax.scipy.linalg.solve_triangular(pivot_factor, panel_rows.T, lower=True).T
        solved = solved.reshape(-1, tile_edge, tile_edge)
        lower_part = jnp.where((block_rows > panel_idx)[:, None, None], solved, 0.0)
        prepare_written = jnp.where(
            (block_rows == panel_idx)[:, None, None], pivot_factor[None], lower_part
        )
        prepare_shared = broadcast(lower_part, "col", panel_idx % grid_cols)
        chosen = lax.dynamic_index_in_dim(
            prepare_shared.reshape(block_count // grid_cols, stride, tile_edge, tile_edge),
            my_col // grid_rows,
            1,
            keepdims=False,
        )
        prepare_across = broadcast(chosen, "row", my_col % grid_rows)
        tiles_now = grid_tiles - jnp.einsum(
            "jab,scb->jsac", prepare_shared, prepare_across, precision=PRECISE
        )
        local_col = panel_idx // grid_cols
        fresh = jnp.where(my_col == panel_idx % grid_cols, prepare_written, tiles_now[:, local_col])
        grid_tiles = tiles_now.at[:, local_col].set(fresh)
    row_grid = block_rows[:, None, None, None]
    col_grid = block_cols[None, :, None, None]
    inside = jnp.arange(tile_edge)[:, None] >= jnp.arange(tile_edge)[None, :]
    keep_mask = (row_grid > col_grid) | (row_grid == col_grid) & inside[None, None]
    result = jnp.where(keep_mask, grid_tiles, 0.0)
    return result.reshape(
        block_count // grid_rows, 1, block_count // grid_cols, 1, tile_edge, tile_edge
    )


def solution(mesh):
    return jax.shard_map(
        local,
        mesh=mesh,
        in_specs=(
            P(None, ("row", "col")),
            P(("row", "col"), None, None),
            P(("row", "col"), None),
            P(("row", "col"), None),
            P(("row", "col"), None),
            P(("row", "col"), None),
        ),
        out_specs=P(None, "row", None, "col", None, None),
        check_vma=False,
    )
```

profile of v0, /device:TPU:12, one launch (start us, length us, event | category | flops | bytes accessed | tf_op | source)
XLA Modules:
  0.0 977.6 jit_solution(2281378333469623732)
XLA Ops:
  6.5 6.0 copy.132
  14.3 10.4 %all-to-all-start = ((s32[128,2,1]{1,2,0:T(1,128)}), s32[128,2,1]{1,2,0:T(1,128)S(1)}, u32[]{:S(2)}, u32[]{:S(2)}) async-start(s32[128,2,1]{1,2,0:T(1,128)} %bitcast.5), calls=%async_computation | async-start | bytes 131072 | tf_op jit(solution)/shard_map/all_to_all | solution.py:46
  24.7 2.3 fusion.1
  27.0 2.3 fusion
  29.3 7.8 broadcast_in_dim.130
  37.2 5.4 scatter_fusion
  42.6 10.2 %all-to-all-start.1 = ((f32[256,128,128]{2,1,0:T(8,128)}), f32[256,128,128]{2,1,0:T(8,128)}, u32[]{:S(2)}, u32[]{:S(2)}) async-start(f32[256,128,128]{2,1,0:T(8,128)} %scatter_fusion), calls=%async_computation.1 | async-start | bytes 33554432 | tf_op jit(solution)/shard_map/all_to_all | solution.py:45
  54.4 240.1 %all-to-all-done.1 = f32[256,128,128]{2,1,0:T(8,128)} async-done(((f32[256,128,128]{2,1,0:T(8,128)}), f32[256,128,128]{2,1,0:T(8,128)}, u32[]{:S(2)}, u32[]{:S(2)}) %all-to-all-start.1) | async-done | bytes 16777248 | tf_op jit(solution)/shard_map/all_to_all | solution.py:45
  294.5 55.0 %scatter_fusion.1 = f32[128,128,128]{2,1,0:T(8,128)} fusion(f32[128,128,128]{2,1,0:T(8,128)} %bitcast.110, s32[256]{0:T(256)S(1)} %reshape.269, f32[256,128,128]{2,1,0:T(8,128)} %all-to-all-done.1), kind=kCustom, calls=%fused_computation.2 | custom fusion | flops 4194304 | bytes 50332672 | tf_op jit(solution)/shard_map/scatter-add | solution.py:49
  349.5 7.7 copy.86
  357.2 9.6 all-to-all-start.2
  366.9 94.6 %all-to-all-done.2 = f32[16,8,128,128]{3,2,0,1:T(8,128)} async-done(((f32[16,8,128,128]{3,2,0,1:T(8,128)}), f32[16,8,128,128]{3,2,0,1:T(8,128)}, u32[]{:S(2)}, u32[]{:S(2)}) %all-to-all-start.2) | async-done | bytes 8388640 | tf_op jit(solution)/shard_map/all_to_all | solution.py:50
  461.5 1.5 fusion.21
  464.6 61.6 %all-reduce.7.cloned.1.call-done = f32[128,128]{1,0:T(8,128)} async-done(((f32[128,128]{1,0:T(8,128)}), f32[128,128]{1,0:T(8,128)}) %all-reduce.7.cloned.1.call-update) | async-done | bytes 65552 | tf_op jit(solution)/shard_map/psum | solution.py:15
  528.2 11.7 %cholesky.44 = f32[128,128]{1,0:T(8,128)S(1)} custom-call(f32[128,128]{1,0:T(8,128)S(1)} %fusion.25), custom_call_target="Cholesky" | custom-call | tf_op jit(solution)/shard_map/jit(cholesky)/cholesky | solution.py:69
  541.3 9.8 %custom-call.6 = f32[1,128,128]{1,2,0:T(8,128)S(1)} custom-call(f32[1,128,128]{2,1,0:T(8,128)S(1)} %get-tuple-element.33), custom_call_target="InvertDiagBlocksLowerTriangular" | custom-call | tf_op jit(solution)/shard_map/jit(_solve_triangular)/triangular_solve | solution.py:71
  553.8 83.9 %all-reduce.9.cloned.1.call-done = f32[16,128,128]{2,1,0:T(8,128)} async-done(((f32[16,128,128]{2,1,0:T(8,128)}), f32[16,128,128]{2,1,0:T(8,128)}) %all-reduce.9.cloned.1.call-update) | async-done | bytes 1048592 | tf_op jit(solution)/shard_map/psum | solution.py:15
  637.7 1.9 fusion.13
  639.7 62.9 %all-reduce.11.cloned.1.call-done = f32[8,128,128]{2,1,0:T(8,128)} async-done(((f32[8,128,128]{2,1,0:T(8,128)}), f32[8,128,128]{2,1,0:T(8,128)}) %all-reduce.11.cloned.1.call-update) | async-done | bytes 524304 | tf_op jit(solution)/shard_map/psum | solution.py:15
  702.6 10.0 %bitcast_subtract_fusion.1 = f32[16,8,128,128]{3,2,1,0:T(8,128)S(1)} fusion(f32[16,128,128]{2,1,0:T(8,128)} %all-reduce.9.cloned.1.call-done, f32[8,128,128]{2,1,0:T(8,128)} %all-reduce.11.cloned.1.call-done, f32[16,8,128,128]{3,2,0,1:T(8,128)} %all-to-all-done.2), kind=kOutput, calls=%fused_computation.4 | convolution fusion | flops 3223322624 | bytes 18350080 | tf_op jit(solution)/shard_map/jab,scb->jsac/dot_general | solution.py:85
  712.7 3.4 copy-done.2
  718.4 1.6 copy.99
  720.0 57.1 %all-reduce.13.cloned.1.call-done = f32[128,128]{1,0:T(8,128)} async-done(((f32[128,128]{1,0:T(8,128)}), f32[128,128]{1,0:T(8,128)}) %all-reduce.13.cloned.1.call-update) | async-done | bytes 65552 | tf_op jit(solution)/shard_map/psum | solution.py:15
  779.1 11.7 %cholesky.55 = f32[128,128]{1,0:T(8,128)S(1)} custom-call(f32[128,128]{1,0:T(8,128)S(1)} %fusion.23), custom_call_target="Cholesky" | custom-call | tf_op jit(solution)/shard_map/jit(cholesky)/cholesky | solution.py:69
  792.3 9.8 %custom-call.7 = f32[1,128,128]{1,2,0:T(8,128)S(1)} custom-call(f32[1,128,128]{2,1,0:T(8,128)S(1)} %get-tuple-element.31), custom_call_target="InvertDiagBlocksLowerTriangular" | custom-call | tf_op jit(solution)/shard_map/jit(_solve_triangular)/triangular_solve | solution.py:71
  802.2 2.4 convolution_bitcast_fusion
  804.5 1.5 copy.100
  807.7 83.7 %all-reduce.15.cloned.1.call-done = f32[16,128,128]{2,1,0:T(8,128)} async-done(((f32[16,128,128]{2,1,0:T(8,128)}), f32[16,128,128]{2,1,0:T(8,128)}) %all-reduce.15.cloned.1.call-update) | async-done | bytes 1048592 | tf_op jit(solution)/shard_map/psum | solution.py:15
  891.4 1.9 fusion.12
  894.4 61.7 %all-reduce.17.cloned.1.call-done = f32[8,128,128]{2,1,0:T(8,128)} async-done(((f32[8,128,128]{2,1,0:T(8,128)}), f32[8,128,128]{2,1,0:T(8,128)}) %all-reduce.17.cloned.1.call-update) | async-done | bytes 524304 | tf_op jit(solution)/shard_map/psum | solution.py:15
  956.1 10.0 %bitcast_subtract_fusion = f32[16,8,128,128]{3,2,1,0:T(8,128)S(1)} fusion(f32[16,8,128,128]{3,2,1,0:T(8,128)} %constant_dynamic-update-slice_fusion, f32[16,128,128]{2,1,0:T(8,128)} %all-reduce.15.cloned.1.call-done, f32[8,128,128]{2,1,0:T(8,128)} %all-reduce.17.cloned.1.call-done), kind=kOutput, calls=%fused_computation.3 | convolution fusion | flops 3223322624 | bytes 18350080 | tf_op jit(solution)/shard_map/jab,scb->jsac/dot_general | solution.py:85
  966.5 4.2 select_bitcast_fusion
  (71 shorter events, 19.7 us)
Async XLA Ops:
  6.5 18.2 %copy-start = (f32[32,128,128]{2,1,0:T(8,128)S(1)}, f32[32,128,128]{2,1,0:T(8,128)}, u32[]{:S(2)}) copy-start(f32[32,128,128]{2,1,0:T(8,128)} %param.14) | copy-start | bytes 6291460
  6.5 6.0 copy-start.5
  6.5 6.2 copy-start.6
  6.5 18.2 %copy-start.3 = (s32[32,128]{1,0:T(8,128)S(1)}, s32[32,128]{1,0:T(8,128)}, u32[]{:S(2)}) copy-start(s32[32,128]{1,0:T(8,128)} %param.16) | copy-start | bytes 49156
  6.5 20.5 %copy-start.4 = (s32[32,128]{1,0:T(8,128)S(1)}, s32[32,128]{1,0:T(8,128)}, u32[]{:S(2)}) copy-start(s32[32,128]{1,0:T(8,128)} %param.15) | copy-start | bytes 49156
  14.3 28.2 %all-to-all-start = ((s32[128,2,1]{1,2,0:T(1,128)}), s32[128,2,1]{1,2,0:T(1,128)S(1)}, u32[]{:S(2)}, u32[]{:S(2)}) async-start(s32[128,2,1]{1,2,0:T(1,128)} %bitcast.5), calls=%async_computation | async-start | bytes 131072 | tf_op jit(solution)/shard_map/all_to_all | solution.py:46
  42.6 251.9 %all-to-all-start.1 = ((f32[256,128,128]{2,1,0:T(8,128)}), f32[256,128,128]{2,1,0:T(8,128)}, u32[]{:S(2)}, u32[]{:S(2)}) async-start(f32[256,128,128]{2,1,0:T(8,128)} %scatter_fusion), calls=%async_computation.1 | async-start | bytes 33554432 | tf_op jit(solution)/shard_map/all_to_all | solution.py:45
  357.2 104.3 %all-to-all-start.2 = ((f32[16,8,128,128]{3,2,0,1:T(8,128)}), f32[16,8,128,128]{3,2,0,1:T(8,128)}, u32[]{:S(2)}, u32[]{:S(2)}) async-start(f32[16,8,128,128]{3,2,0,1:T(8,128)} %copy.86), calls=%async_computation.2 | async-start | bytes 16777216 | tf_op jit(solution)/shard_map/all_to_all | solution.py:50
  366.8 159.4 %all-reduce.7.cloned.1.call-start = ((), (), s32[]{:S(2)}) async-start(), calls=%async_computation.3 | async-start | bytes 131072 | tf_op jit(solution)/shard_map/psum | solution.py:15
  463.0 174.7 %all-reduce.9.cloned.1.call-start = ((), (), s32[]{:S(2)}) async-start(), calls=%async_computation.4 | async-start | bytes 2097152 | tf_op jit(solution)/shard_map/psum | solution.py:15
  553.7 149.0 %all-reduce.11.cloned.1.call-start = ((), (), s32[]{:S(2)}) async-start(), calls=%async_computation.5 | async-start | bytes 1048576 | tf_op jit(solution)/shard_map/psum | solution.py:15
  639.6 137.5 %all-reduce.13.cloned.1.call-start = ((), (), s32[]{:S(2)}) async-start(), calls=%async_computation.6 | async-start | bytes 131072 | tf_op jit(solution)/shard_map/psum | solution.py:15
  712.7 3.4 copy-start.2
  717.9 173.5 %all-reduce.15.cloned.1.call-start = ((), (), s32[]{:S(2)}) async-start(), calls=%async_computation.7 | async-start | bytes 2097152 | tf_op jit(solution)/shard_map/psum | solution.py:15
  807.3 148.8 %all-reduce.17.cloned.1.call-start = ((), (), s32[]{:S(2)}) async-start(), calls=%async_computation.8 | async-start | bytes 1048576 | tf_op jit(solution)/shard_map/psum | solution.py:15
  966.5 4.3 copy-start.1
Sparse Core Ops, SparseCore 0:
  463.1 63.0 all-reduce.6
  553.8 83.8 all-reduce.8
  640.0 62.5 all-reduce.10
  718.0 59.0 all-reduce.12
  807.4 83.8 all-reduce.14
  893.6 62.5 all-reduce.16
where the time goes:
time: 979 us; the launch traced here: 978 us
  waiting for transfers between devices  746 us (76%)
  other arithmetic  119 us (12%)
  local copies, waits for them, and re-layouts  39.8 us (4%)
  starting transfers between devices  31.2 us (3%)
  matrix products  28.1 us (3%)
  between operations  13.9 us (1%)
    psum x6, waiting for transfers between devices, broadcast(): return lax.psum(kept, axis)  411 us
    all_to_all x1, waiting for transfers between devices, local(): lax.all_to_all(outgoing, ('row', 'col'), split_axis=0, concat_axis=0, til...  240 us
    all_to_all x1, waiting for transfers between devices, local(): lax.all_to_all(column_blocks.reshape(block_count // grid_rows, grid_rows,...  94.6 us
    scatter-add x1, other arithmetic, local(): jax.ops.segment_sum(arrived, landing, num_segments=block_count)  55 us
    another operation x6, other arithmetic, local(): pivot_factor = jnp.linalg.cholesky(symmetric)  24.9 us
    another operation x4, other arithmetic, local(): jax.scipy.linalg.solve_triangular(pivot_factor, panel_rows.T, lower=True)  21 us
    dot_general x2, matrix products, local(): jnp.einsum('jab,scb->jsac', prepare_shared, prepare_across, precision=PRE...  20.1 us
  transfers between devices with their start and end apart: 9, of which 8 were waited for; matrix products, arithmetic and copies ran while one was open for 2% of the time, Pallas kernels for 0%

commit v1 on v0

v1 whole, which is shorter than its diff:
```python
import functools

import jax
import jax.numpy as jnp
from jax import lax
from jax.experimental import pallas as pl
from jax.experimental.pallas import tpu as pltpu
from jax.sharding import PartitionSpec as P

SLOTS = 2
EDGE = 128
MESH = pl.DeviceIdType.MESH
PRECISE = lax.Precision.HIGHEST
F32 = jnp.float32


def dot(a, b, dims):
    return lax.dot_general(a, b, (dims, ((), ())), precision=PRECISE, preferred_element_type=F32)


NN = ((1,), (0,))
NT = ((1,), (1,))
TN = ((0,), (0,))


def pack_kernel(position, tile, row_map, col_map, out):
    t = pl.program_id(0)
    levels = lax.broadcasted_iota(jnp.int32, (EDGE, EDGE), 0)
    col_hot = (levels == col_map[pl.ds(t, 1), :]).astype(F32)
    row_hot = (levels == row_map[pl.ds(t, 1), :]).astype(F32)
    half = dot(tile[0], col_hot, NT)
    out[0] = dot(row_hot, half, NN)


def pack(position, tiles, row_map, col_map, slots):
    count = tiles.shape[0]
    whole = pl.BlockSpec((count, EDGE), lambda t, pos: (0, 0))
    return pl.pallas_call(
        pack_kernel,
        grid_spec=pltpu.PrefetchScalarGridSpec(
            num_scalar_prefetch=1,
            grid=(count,),
            in_specs=[pl.BlockSpec((1, EDGE, EDGE), lambda t, pos: (t, 0, 0)), whole, whole],
            out_specs=pl.BlockSpec((1, EDGE, EDGE), lambda t, pos: (pos[t], 0, 0)),
        ),
        out_shape=jax.ShapeDtypeStruct((slots, EDGE, EDGE), F32),
        name="pack",
    )(position, tiles, row_map, col_map)


DEPTH = 8


def gather_kernel(landing, front, arrived, out, acc, ring, index, sem, ring_sem):
    slots = arrived.shape[0]
    load = pltpu.make_async_copy(front, acc, sem)
    load.start()

    def note(k, n):
        valid = landing[k] >= 0

        @pl.when(valid)
        def _():
            index[n] = k

        return n + valid.astype(jnp.int32)

    count = lax.fori_loop(0, slots, note, 0)

    def fetch(k):
        slot = lax.rem(k, DEPTH)
        return pltpu.make_async_copy(arrived.at[index[k]], ring.at[slot], ring_sem.at[slot])

    def prime(k, _):
        fetch(k).start()
        return 0

    lax.fori_loop(0, jnp.minimum(count, DEPTH), prime, 0)
    load.wait()

    def step(k, _):
        fetch(k).wait()
        where = landing[index[k]]
        acc[where] = acc[where] + ring[lax.rem(k, DEPTH)]

        @pl.when(k + DEPTH < count)
        def _():
            fetch(k + DEPTH).start()

        return 0

    lax.fori_loop(0, count, step, 0)
    store = pltpu.make_async_copy(acc, out, sem)
    store.start()
    store.wait()


def gather(landing, front, arrived):
    hbm = pl.BlockSpec(memory_space=pltpu.HBM)
    return pl.pallas_call(
        gather_kernel,
        in_specs=[pl.BlockSpec(memory_space=pltpu.SMEM), hbm, hbm],
        out_specs=hbm,
        out_shape=jax.ShapeDtypeStruct(front.shape, F32),
        scratch_shapes=[
            pltpu.VMEM(front.shape, F32),
            pltpu.VMEM((DEPTH, EDGE, EDGE), F32),
            pltpu.SMEM(landing.shape, jnp.int32),
            pltpu.SemaphoreType.DMA,
            pltpu.SemaphoreType.DMA((DEPTH,)),
        ],
        compiler_params=pltpu.CompilerParams(vmem_limit_bytes=32 << 20),
        name="gather",
    )(landing, front, arrived)


STEP = 8


def factor(work, upper):
    rows8 = lax.broadcasted_iota(jnp.int32, (STEP, 2 * EDGE), 0)
    lanes = lax.broadcasted_iota(jnp.int32, (STEP, EDGE), 1)

    def block(b, _):
        first = pl.multiple_of(b * STEP, STEP)
        x = work[pl.ds(first, STEP), :]
        d = pltpu.roll(x[:, :EDGE], lax.rem(EDGE - first, EDGE), 1)
        for t in range(STEP):
            pivot = d[t : t + 1, t : t + 1]
            scale = lax.rsqrt(pivot)
            ratio = d[:, t : t + 1] / pivot
            below = rows8[:, :1] > t
            at = rows8[:, :1] == t
            ratio = jnp.where(below, ratio, jnp.where(at, 1.0 - scale, 0.0))
            x = x - ratio * x[t : t + 1, :]
            d = d - ratio * d[t : t + 1, :]
        upper[pl.ds(first, STEP), :] = x
        left = jnp.where(lanes >= first + STEP, x[:, :EDGE], 0.0)
        work[...] = work[...] - dot(left, x, TN)
        return 0

    lax.fori_loop(0, EDGE // STEP, block, 0)


def panel_kernel(
    R, C, col, grid, qrow, qcol,
    stage, diag, chunk, qc, qrow_v, work, upper, low,
    st_in, st_out, b_send, b_recv, dgr_send, dgc_send, dg_recv, sc_send, ck_recv,
    ag_send, ag_recv, rl_send, rl_recv, out_sem, qc_sem,
):
    r = lax.axis_index("row")
    c = lax.axis_index("col")
    NB = R * C
    ratio = C // R
    j = r * C + c
    start_of = lambda column: jnp.where(column < 2, 0, column)
    i0 = start_of(j)

    def remote(src, dst, ss, rs, rr, cc):
        return pltpu.make_async_remote_copy(
            src_ref=src, dst_ref=dst, send_sem=ss, recv_sem=rs, device_id=(rr, cc), device_id_type=MESH
        )

    barrier = pltpu.get_barrier_semaphore()
    for k in range(1, R):
        pl.semaphore_signal(barrier, inc=1, device_id=(lax.rem(r + k, R), c), device_id_type=MESH)
    for k in range(1, C):
        pl.semaphore_signal(barrier, inc=1, device_id=(r, lax.rem(c + k, C)), device_id_type=MESH)
    pl.semaphore_wait(barrier, R + C - 2)

    pieces = ((0, 0, 2), (1, 2, 1))

    def diag_row(p, k):
        owner, at, n = pieces[p]
        return remote(
            col.at[pl.ds(owner, n)], diag.at[pl.ds(at, n)], dgr_send.at[k], dg_recv.at[p], lax.rem(r + k, R), c
        )

    def diag_col(p, k):
        owner, at, n = pieces[p]
        here = diag.at[pl.ds(at, n)]
        return remote(here, here, dgc_send.at[k], dg_recv.at[p], r, lax.rem(c + k, C))

    def diag_own(p):
        owner, at, n = pieces[p]
        return pltpu.make_async_copy(col.at[pl.ds(owner, n)], diag.at[pl.ds(at, n)], dg_recv.at[p])

    for p in range(2):

        @pl.when((r == 0) & (c == pieces[p][0]))
        def _():
            for k in range(1, R):
                diag_row(p, k).start()
            diag_own(p).start()

    def b_copy(i):
        return remote(
            col.at[i], grid.at[i // R, r], b_send.at[i], b_recv.at[i // R, r], lax.rem(i, R), c
        )

    def b_wait(jl, s):
        remote(col.at[0], grid.at[jl, s], b_send.at[0], b_recv.at[jl, s], r, c).wait_recv()

    def own_in(jl):
        return pltpu.make_async_copy(col.at[jl * R + r], stage.at[jl], st_in.at[jl])

    def own_out(jl):
        return pltpu.make_async_copy(stage.at[jl], grid.at[jl, r], st_out.at[jl])

    def over(low_end, high_end, body):
        def run(i, _):
            body(i)
            return 0

        lax.fori_loop(low_end, high_end, run, 0)

    def own_blocks(body):
        def run(jl):
            @pl.when(jl * R + r >= i0)
            def _():
                body(jl)

        over(0, C, run)

    def sent_blocks(body):
        def run(i):
            @pl.when(lax.rem(i, R) != r)
            def _():
                body(i)

        over(i0, NB, run)

    late = (r == 1) & (c < 2)
    own_blocks(lambda jl: own_in(jl).start())

    @pl.when(jnp.logical_not(late))
    def _():
        sent_blocks(lambda i: b_copy(i).start())

    def own_turn(jl):
        own_in(jl).wait()
        own_out(jl).start()

    own_blocks(own_turn)

    def diag_wait(p):
        diag_own(p).wait()

    for p in range(2):

        @pl.when(c == pieces[p][0])
        def _():
            diag_wait(p)
            for k in range(1, C):
                diag_col(p, k).start()

    for p in range(2):

        @pl.when(c != pieces[p][0])
        def _():
            diag_wait(p)

    rows = lax.broadcasted_iota(jnp.int32, (EDGE, EDGE), 0)
    cols = lax.broadcasted_iota(jnp.int32, (EDGE, EDGE), 1)
    eye = (rows == cols).astype(F32)

    def pivot(block, at):
        work[:, :EDGE] = jnp.where(rows >= cols, block, block.T)
        work[:, EDGE:] = eye
        factor(work, upper)
        low[at] = jnp.where(rows >= cols, upper[:, :EDGE].T, 0.0)
        low[at + 1] = jnp.where(rows >= cols, upper[:, EDGE:], 0.0)

    pivot(diag[0], 0)
    low[2] = dot(diag[1], low[1], NT)
    pivot(diag[2] - dot(low[2], low[2], NT), 3)

    def scatter(jl, k):
        return remote(grid.at[jl, 0], chunk.at[k], sc_send.at[jl], ck_recv.at[k], r, jl)

    def scatter_own(jl, k):
        return pltpu.make_async_copy(grid.at[jl, 0], chunk.at[k], ck_recv.at[k])

    for k in range(2):

        @pl.when(c == k)
        def _():
            def run(jl):
                @pl.when(r == 0)
                def _():
                    own_out(jl).wait()

                @pl.when(r != 0)
                def _():
                    b_wait(jl, 0)

                @pl.when(jl == c)
                def _():
                    scatter_own(jl, k).start()

                @pl.when(jl != c)
                def _():
                    scatter(jl, k).start()

            over(0, C, run)

    @pl.when(late)
    def _():
        sent_blocks(lambda i: b_copy(i).start())

    scatter_own(0, 0).wait()
    scatter_own(0, 1).wait()

    i = c * R + r
    q0 = dot(chunk[0], low[1], NT)
    q1 = dot(chunk[1] - dot(q0, low[2], NT), low[4], NT)
    q0 = jnp.where(i == 0, low[0], jnp.where(i == 1, low[2], q0))
    q1 = jnp.where(i == 0, 0.0, jnp.where(i == 1, low[3], q1))
    qc[:, :EDGE] = q0
    qc[:, EDGE:] = q1

    def spread(k):
        return remote(qc, qrow_v.at[c], ag_send.at[k], ag_recv.at[c], r, lax.rem(c + k, C))

    own_q = pltpu.make_async_copy(qc, qrow_v.at[c], qc_sem)
    own_q.start()
    for k in range(1, C):
        spread(k).start()
    own_q.wait()

    def spread_wait(jl):
        @pl.when(jl != c)
        def _():
            remote(qc, qrow_v.at[jl], ag_send.at[0], ag_recv.at[jl], r, c).wait_recv()

    over(0, C, spread_wait)

    source = lax.rem(c, R)

    def relay(s, k):
        jl = s * ratio + c // R
        return remote(
            qrow_v.at[jl], qcol.at[s], rl_send.at[s, k], rl_recv.at[s], lax.rem(r + k, R), c
        )

    def relay_own(s):
        return pltpu.make_async_copy(qrow_v.at[s * ratio + c // R], qcol.at[s], rl_recv.at[s])

    @pl.when(r == source)
    def _():
        def run(s):
            for k in range(1, R):
                relay(s, k).start()
            relay_own(s).start()

        over(0, R, run)

    keep = pltpu.make_async_copy(qrow_v, qrow, out_sem)
    keep.start()

    over(0, R, lambda s: relay_own(s).wait())
    keep.wait()

    for s in range(R):
        begin = start_of(s * C + c)

        def run(jl):
            @pl.when((r != s) & (jl * R + r >= begin))
            def _():
                b_wait(jl, s)

        if s == 0:

            @pl.when(c >= 2)
            def _():
                over(0, C, run)
        else:
            over(0, C, run)

    @pl.when((r != 0) | (c >= 2))
    def _():
        own_blocks(lambda jl: own_out(jl).wait())

    sent_blocks(lambda i: b_copy(i).wait_send())

    for p in range(2):

        @pl.when((r == 0) & (c == pieces[p][0]))
        def _():
            for k in range(1, R):
                diag_row(p, k).wait_send()

        @pl.when(c == pieces[p][0])
        def _():
            for k in range(1, C):
                diag_col(p, k).wait_send()

    for k in range(2):

        @pl.when(c == k)
        def _():
            def run(jl):
                @pl.when(jl != c)
                def _():
                    scatter(jl, k).wait_send()

            over(0, C, run)

    for k in range(1, C):
        spread(k).wait_send()

    @pl.when(r == source)
    def _():
        def run(s):
            for k in range(1, R):
                relay(s, k).wait_send()

        over(0, R, run)


def panels(R, C, column):
    hbm = pl.BlockSpec(memory_space=pltpu.HBM)
    dma = pltpu.SemaphoreType.DMA
    return pl.pallas_call(
        functools.partial(panel_kernel, R, C),
        in_specs=[hbm],
        out_specs=[hbm, hbm, hbm],
        out_shape=[
            jax.ShapeDtypeStruct((C, R, EDGE, EDGE), F32),
            jax.ShapeDtypeStruct((C, EDGE, 2 * EDGE), F32),
            jax.ShapeDtypeStruct((R, EDGE, 2 * EDGE), F32),
        ],
        scratch_shapes=[
            pltpu.VMEM((C, EDGE, EDGE), F32),
            pltpu.VMEM((3, EDGE, EDGE), F32),
            pltpu.VMEM((2, EDGE, EDGE), F32),
            pltpu.VMEM((EDGE, 2 * EDGE), F32),
            pltpu.VMEM((C, EDGE, 2 * EDGE), F32),
            pltpu.VMEM((EDGE, 2 * EDGE), F32),
            pltpu.VMEM((EDGE, 2 * EDGE), F32),
            pltpu.VMEM((5, EDGE, EDGE), F32),
            dma((C,)), dma((C,)), dma((R * C,)), dma((C, R)),
            dma((R,)), dma((C,)), dma((2,)), dma((C,)), dma((2,)),
            dma((C,)), dma((C,)), dma((R, R)), dma((R,)), dma, dma,
        ],
        compiler_params=pltpu.CompilerParams(
            collective_id=0, has_side_effects=True, vmem_limit_bytes=32 << 20
        ),
        name="panels",
    )(column)


def update_kernel(R, C, place, grid, qrow, qcol, out):
    jl = pl.program_id(0)
    r, c = place[0], place[1]
    i = jl * R + r
    rows = lax.broadcasted_iota(jnp.int32, (EDGE, EDGE), 0)
    cols = lax.broadcasted_iota(jnp.int32, (EDGE, EDGE), 1)
    for s in range(R):
        j = s * C + c

        @pl.when(i < j)
        def _():
            out[0, s] = jnp.zeros((EDGE, EDGE), F32)

        @pl.when((i >= j) & (j < 2))
        def _():
            out[0, s] = jnp.where(j == 0, qrow[0, :, :EDGE], qrow[0, :, EDGE:])

        @pl.when((i >= j) & (j >= 2))
        def _():
            fresh = grid[0, s] - dot(qrow[0], qcol[s], NT)
            out[0, s] = jnp.where((i > j) | (rows >= cols), fresh, 0.0)


def update(R, C, place, grid, qrow, qcol):
    wide = pl.BlockSpec((1, R, EDGE, EDGE), lambda jl, place: (jl, 0, 0, 0))
    return pl.pallas_call(
        functools.partial(update_kernel, R, C),
        grid_spec=pltpu.PrefetchScalarGridSpec(
            num_scalar_prefetch=1,
            grid=(C,),
            in_specs=[
                wide,
                pl.BlockSpec((1, EDGE, 2 * EDGE), lambda jl, place: (jl, 0, 0)),
                pl.BlockSpec((R, EDGE, 2 * EDGE), lambda jl, place: (0, 0, 0)),
            ],
            out_specs=wide,
        ),
        out_shape=jax.ShapeDtypeStruct((C, R, EDGE, EDGE), F32),
        name="update",
    )(place, grid, qrow, qcol)


def local(front_entries, child_updates, row_maps, col_maps, target_columns, row_offsets):
    R = lax.axis_size("row")
    C = lax.axis_size("col")
    count = R * C
    held = child_updates.shape[0]
    columns = target_columns[:, 0]
    offsets = row_offsets[:, 0]
    target_rows = columns + offsets % (count - columns)
    serial = jnp.arange(held, dtype=jnp.int32)
    earlier = (columns[:, None] == columns[None, :]) & (serial[None, :] < serial[:, None])
    position = columns * SLOTS + jnp.sum(earlier.astype(jnp.int32), axis=1)
    hit = position[:, None] == jnp.arange(count * SLOTS, dtype=jnp.int32)[None, :]
    targets = jnp.max(jnp.where(hit, target_rows[:, None], -1), axis=0)
    outgoing = pack(position, child_updates, row_maps, col_maps, count * SLOTS)
    landing = lax.all_to_all(targets, ("row", "col"), split_axis=0, concat_axis=0, tiled=True)
    arrived = lax.all_to_all(outgoing, ("row", "col"), split_axis=0, concat_axis=0, tiled=True)
    column = gather(landing, front_entries.reshape(count, EDGE, EDGE), arrived)
    grid, qrow, qcol = panels(R, C, column)
    place = jnp.stack([lax.axis_index("row"), lax.axis_index("col")]).astype(jnp.int32)
    result = update(R, C, place, grid, qrow, qcol)
    return result.reshape(C, 1, R, 1, EDGE, EDGE)


def solution(mesh):
    return jax.shard_map(
        local,
        mesh=mesh,
        in_specs=(
            P(None, ("row", "col")),
            P(("row", "col"), None, None),
            P(("row", "col"), None),
            P(("row", "col"), None),
            P(("row", "col"), None),
            P(("row", "col"), None),
        ),
        out_specs=P(None, "row", None, "col", None, None),
        check_vma=False,
    )
```

time: 979 us -> 525 us (0.54)
  the two profiles are of different devices: /device:TPU:12 before, /device:TPU:25 now
where the time goes in v1:
time: 525 us; the launch traced here: 521 us
  Pallas kernels  267 us (51%)
  waiting for transfers between devices  219 us (42%)
  starting transfers between devices  20.8 us (4%)
  local copies, waits for them, and re-layouts  10.4 us (2%)
    all_to_all x1, waiting for transfers between devices, local(): lax.all_to_all(outgoing, ('row', 'col'), split_axis=0, concat_axis=0, til...  219 us
    pallas_call x1, Pallas kernels, panels(): pl.pallas_call(functools.partial(panel_kernel, R, C), in_specs=[hbm], out...  211 us
    pallas_call x1, Pallas kernels, pack(): pl.pallas_call(pack_kernel, grid_spec=pltpu.PrefetchScalarGridSpec(num_sc...  24.5 us
    pallas_call x1, Pallas kernels, update(): pl.pallas_call(functools.partial(update_kernel, R, C), grid_spec=pltpu.Pr...  23.7 us
    all_to_all x1, starting transfers between devices, local(): lax.all_to_all(targets, ('row', 'col'), split_axis=0, concat_axis=0, tile...  10.6 us
  transfers between devices with their start and end apart: 2, of which 1 were waited for; matrix products, arithmetic and copies ran while one was open for 1% of the time, Pallas kernels for 5%

profile of v1, /device:TPU:25, one launch (start us, length us, event | category | flops | bytes accessed | tf_op | source)
XLA Modules:
  0.0 521.1 jit_solution(14832947940668514168)
XLA Ops:
  0.0 0.9 convert_reduce_fusion
  0.9 0.8 fusion.2
  1.7 0.1 select_reduce_fusion
  1.8 0.8 all_to_all.10
  2.6 10.6 %all-to-all-start = ((s32[128,2,1]{1,2,0:T(1,128)}), s32[128,2,1]{1,2,0:T(1,128)S(1)}, u32[]{:S(2)}, u32[]{:S(2)}) async-start(s32[128,2,1]{1,2,0:T(1,128)} %bitcast.6), calls=%async_computation | async-start | bytes 131072 | tf_op jit(solution)/shard_map/all_to_all | solution.py:509
  13.1 1.2 multiply_add_fusion.position
  14.3 24.5 %pack.1 = f32[256,128,128]{2,1,0:T(8,128)} custom-call(s32[32]{0:T(128)} %multiply_add_fusion.position, f32[32,128,128]{2,1,0:T(8,128)} %tile.1, s32[32,128]{1,0:T(8,128)} %row_map.1, s32[32,128]{1,0:T(8,128)} %col_map.1), custom_call_target="tpu_custom_call" | custom-call | tf_op jit(solution)/shard_map/pack/pallas_call | solution.py:38
  38.8 0.0 all-to-all-done
  38.8 10.2 %all-to-all-start.1 = ((f32[256,128,128]{2,1,0:T(8,128)}), f32[256,128,128]{2,1,0:T(8,128)}, u32[]{:S(2)}, u32[]{:S(2)}) async-start(f32[256,128,128]{2,1,0:T(8,128)} %pack.1), calls=%async_computation.1 | async-start | bytes 33554432 | tf_op jit(solution)/shard_map/all_to_all | solution.py:510
  49.1 0.7 pad_add_fusion.place
  49.8 0.5 broadcast.12
  50.3 0.8 reduce.3
  51.1 0.1 all_to_all.12.landing
  51.2 218.9 %all-to-all-done.1.arrived = f32[256,128,128]{2,1,0:T(8,128)} async-done(((f32[256,128,128]{2,1,0:T(8,128)}), f32[256,128,128]{2,1,0:T(8,128)}, u32[]{:S(2)}, u32[]{:S(2)}) %all-to-all-start.1) | async-done | bytes 16777248 | tf_op jit(solution)/shard_map/all_to_all | solution.py:510
  270.1 0.0 copy-start
  270.1 3.4 copy-done
  273.5 7.2 %gather.1.col = f32[128,128,128]{2,1,0:T(8,128)S(1)} custom-call(s32[256]{0:T(256)S(1)} %all_to_all.12.landing, f32[128,128,128]{2,1,0:T(8,128)S(1)} %bitcast.18, f32[256,128,128]{2,1,0:T(8,128)} %all-to-all-done.1.arrived), custom_call_target="tpu_custom_call" | custom-call | tf_op jit(solution)/shard_map/gather/pallas_call | solution.py:100
  280.7 211.1 %panels.1 = (f32[16,8,128,128]{3,2,1,0:T(8,128)S(1)}, f32[16,128,256]{2,1,0:T(8,128)S(1)}, f32[8,128,256]{2,1,0:T(8,128)S(1)}) custom-call(f32[128,128,128]{2,1,0:T(8,128)S(1)} %gather.1.col), custom_call_target="tpu_custom_call" | custom-call | tf_op jit(solution)/shard_map/panels/pallas_call | solution.py:424
  491.8 0.0 copy-start.1
  491.8 3.2 copy-done.1
  495.0 0.0 copy-start.2
  495.0 1.4 copy-done.2
  496.4 0.0 copy-start.3
  496.4 1.0 copy-done.3
  497.3 23.7 %update.1 = f32[16,8,128,128]{3,2,1,0:T(8,128)} custom-call(s32[2]{0:T(128)} %pad_add_fusion.place, f32[16,8,128,128]{3,2,1,0:T(8,128)} %copy-done.1, f32[16,128,256]{2,1,0:T(8,128)} %copy-done.2, f32[8,128,256]{2,1,0:T(8,128)} %copy-done.3), custom_call_target="tpu_custom_call" | custom-call | tf_op jit(solution)/shard_map/update/pallas_call | solution.py:478
Async XLA Ops:
  2.6 36.3 %all-to-all-start = ((s32[128,2,1]{1,2,0:T(1,128)}), s32[128,2,1]{1,2,0:T(1,128)S(1)}, u32[]{:S(2)}, u32[]{:S(2)}) async-start(s32[128,2,1]{1,2,0:T(1,128)} %bitcast.6), calls=%async_computation | async-start | bytes 131072 | tf_op jit(solution)/shard_map/all_to_all | solution.py:509
  38.8 231.2 %all-to-all-start.1 = ((f32[256,128,128]{2,1,0:T(8,128)}), f32[256,128,128]{2,1,0:T(8,128)}, u32[]{:S(2)}, u32[]{:S(2)}) async-start(f32[256,128,128]{2,1,0:T(8,128)} %pack.1), calls=%async_computation.1 | async-start | bytes 33554432 | tf_op jit(solution)/shard_map/all_to_all | solution.py:510
  270.1 3.4 copy-start
  491.8 3.2 copy-start.1
  495.0 1.4 copy-start.2
  496.4 1.0 copy-start.3

commit v2 on v0

v2 whole, which is shorter than its diff:
```python
import functools
import math

import jax
import jax.numpy as jnp
from jax import lax
from jax.experimental import pallas as pl
from jax.experimental.pallas import tpu as pltpu
from jax.sharding import PartitionSpec as P

EDGE = 128
MESH = pl.DeviceIdType.MESH
PRECISE = lax.Precision.HIGHEST
F32 = jnp.float32
BF16 = jnp.bfloat16
NN = ((1,), (0,))
NT = ((1,), (1,))
TN = ((0,), (0,))


def dot(a, b, dims):
    return lax.dot_general(a, b, (dims, ((), ())), precision=PRECISE, preferred_element_type=F32)


def dot16(a, b, dims):
    return lax.dot_general(a, b, (dims, ((), ())), preferred_element_type=F32)


def remote(src, dst, ss, rs, rr, cc):
    return pltpu.make_async_remote_copy(
        src_ref=src, dst_ref=dst, send_sem=ss, recv_sem=rs, device_id=(rr, cc), device_id_type=MESH
    )


def over(low, high, body):
    def run(i, _):
        body(i)
        return 0

    lax.fori_loop(low, high, run, 0)


def greet(R, C, r, c):
    barrier = pltpu.get_barrier_semaphore()
    for k in range(1, R):
        pl.semaphore_signal(barrier, inc=1, device_id=(lax.rem(r + k, R), c), device_id_type=MESH)
    for k in range(1, C):
        pl.semaphore_signal(barrier, inc=1, device_id=(r, lax.rem(c + k, C)), device_id_type=MESH)
    pl.semaphore_wait(barrier, R + C - 2)


GROUP = 4


def place_kernel(C, tile, row_map, col_map, out):
    t = pl.program_id(0)
    levels = lax.broadcasted_iota(jnp.int32, (EDGE, EDGE), 0)
    for g in range(GROUP):
        k = t * GROUP + g
        col_hot = (levels == col_map[pl.ds(k, 1), :]).astype(F32).astype(BF16)
        row_hot = (levels == row_map[pl.ds(k, 1), :]).astype(F32).astype(BF16)
        x = tile[g]
        first = x.astype(BF16)
        rest = x - first.astype(F32)
        second = rest.astype(BF16)
        third = (rest - second.astype(F32)).astype(BF16)
        parts = [dot16(p, col_hot, NT).astype(BF16) for p in (first, second, third)]
        placed = (
            dot16(row_hot, parts[0], NN) + dot16(row_hot, parts[1], NN)
        ) + dot16(row_hot, parts[2], NN)
        for q in range(C):
            out[q, g] = placed[q * (EDGE // C) : (q + 1) * (EDGE // C), :]


def place_tiles(C, tiles, row_map, col_map):
    count = tiles.shape[0]
    whole = pl.BlockSpec((count, EDGE), lambda t: (0, 0))
    return pl.pallas_call(
        functools.partial(place_kernel, C),
        grid=(count // GROUP,),
        in_specs=[pl.BlockSpec((GROUP, EDGE, EDGE), lambda t: (t, 0, 0)), whole, whole],
        out_specs=pl.BlockSpec((C, GROUP, EDGE // C, EDGE), lambda t: (0, t, 0, 0)),
        out_shape=jax.ShapeDtypeStruct((C, count, EDGE // C, EDGE), F32),
        name="place",
    )(tiles, row_map, col_map)


def spread_kernel(
    R, C, cap2, cap3, placed, index2, index3, col, grid, out,
    r1, s2, r2, s3, stage,
    st_in, st_out, b_send, b_recv, p1_send, p1_recv, p2_send, p2_recv, p3_send, p3_recv,
):
    r = lax.axis_index("row")
    c = lax.axis_index("col")
    NB = R * C
    T = placed.shape[1]
    start_of = lambda column: jnp.where(column < 2, 0, column)
    i0 = start_of(r * C + c)
    greet(R, C, r, c)

    def first(k):
        to = lax.rem(c + k, C)
        return remote(placed.at[to], r1.at[pl.ds(c * T, T)], p1_send.at[k], p1_recv.at[c], r, to)

    def first_wait(k):
        src = lax.rem(c + k, C)
        remote(placed.at[0], r1.at[pl.ds(src * T, T)], p1_send.at[0], p1_recv.at[src], r, c).wait_recv()

    first_own = pltpu.make_async_copy(placed.at[c], r1.at[pl.ds(c * T, T)], p1_recv.at[c])
    first_own.start()
    for k in range(1, C):
        first(k).start()

    def b_copy(i):
        return remote(
            col.at[i], grid.at[i // R, r], b_send.at[i], b_recv.at[i // R, r], lax.rem(i, R), c
        )

    def own_in(jl):
        return pltpu.make_async_copy(col.at[jl * R + r], stage.at[jl], st_in.at[jl])

    def own_out(jl):
        return pltpu.make_async_copy(stage.at[jl], grid.at[jl, r], st_out.at[jl])

    def own_blocks(body):
        def run(jl):
            @pl.when(jl * R + r >= i0)
            def _():
                body(jl)

        over(0, C, run)

    def sent_blocks(low, high, body):
        def run(i):
            @pl.when(lax.rem(i, R) != r)
            def _():
                body(i)

        over(low, high, run)

    middle = i0 + (NB - i0) // 4
    own_blocks(lambda jl: own_in(jl).start())
    sent_blocks(i0, middle, lambda i: b_copy(i).start())

    def own_turn(jl):
        own_in(jl).wait()
        own_out(jl).start()

    own_blocks(own_turn)

    first_own.wait()
    for k in range(1, C):
        first_wait(k)

    def second(k):
        to = lax.rem(r + k, R)
        return remote(s2.at[to], r2.at[pl.ds(r * cap2, cap2)], p2_send.at[k], p2_recv.at[r], to, c)

    def second_wait(k):
        src = lax.rem(r + k, R)
        remote(s2.at[0], r2.at[pl.ds(src * cap2, cap2)], p2_send.at[0], p2_recv.at[src], r, c).wait_recv()

    UNROLL = 8

    def pack2(k):
        to = lax.rem(r + k, R)

        def run(n):
            for u in range(UNROLL):
                s2[to, n * UNROLL + u] = r1[index2[to * cap2 + n * UNROLL + u]]

        over(0, cap2 // UNROLL, run)

    for k in range(1, R):
        pack2(k)
        if k > 1:
            second(k - 1).start()

    def pack2_own(n):
        for u in range(UNROLL):
            r2[r * cap2 + n * UNROLL + u] = r1[index2[r * cap2 + n * UNROLL + u]]

    over(0, cap2 // UNROLL, pack2_own)
    second(R - 1).start()
    sent_blocks(middle, NB, lambda i: b_copy(i).start())

    for k in range(1, R):
        second_wait(k)

    def third(k):
        to = lax.rem(c + k, C)
        return remote(s3.at[to], out.at[c], p3_send.at[k], p3_recv.at[c], r, to)

    def third_wait(k):
        src = lax.rem(c + k, C)
        remote(s3.at[0], out.at[src], p3_send.at[0], p3_recv.at[src], r, c).wait_recv()

    third_own = pltpu.make_async_copy(s3.at[c], out.at[c], p3_recv.at[c])

    def pack3(k):
        to = lax.rem(c + k, C)

        def run(n):
            for u in range(UNROLL):
                s3[to, n * UNROLL + u] = r2[index3[to * cap3 + n * UNROLL + u]]

        over(0, cap3 // UNROLL, run)

    for k in range(1, C):
        pack3(k)
        if k > 1:
            third(k - 1).start()
    pack3(C)
    third(C - 1).start()

    own_blocks(lambda jl: own_out(jl).wait())
    for s in range(R):
        begin = start_of(s * C + c)

        def run(jl):
            @pl.when((r != s) & (jl * R + r >= begin))
            def _():
                remote(col.at[0], grid.at[jl, s], b_send.at[0], b_recv.at[jl, s], r, c).wait_recv()

        over(0, C, run)
    third_own.start()
    sent_blocks(i0, NB, lambda i: b_copy(i).wait_send())
    for k in range(1, C):
        first(k).wait_send()
    for k in range(1, R):
        second(k).wait_send()
    for k in range(1, C):
        third_wait(k)
    for k in range(1, C):
        third(k).wait_send()
    third_own.wait()


def spread(R, C, cap2, cap3, placed, index2, index3, front):
    hbm = pl.BlockSpec(memory_space=pltpu.HBM)
    smem = pl.BlockSpec(memory_space=pltpu.SMEM)
    dma = pltpu.SemaphoreType.DMA
    T, sub = placed.shape[1], placed.shape[2]
    return pl.pallas_call(
        functools.partial(spread_kernel, R, C, cap2, cap3),
        in_specs=[hbm, smem, smem, hbm],
        out_specs=[hbm, hbm],
        out_shape=[
            jax.ShapeDtypeStruct((C, R, EDGE, EDGE), F32),
            jax.ShapeDtypeStruct((C, cap3, sub, EDGE), F32),
        ],
        scratch_shapes=[
            pltpu.VMEM((C * T, sub, EDGE), F32),
            pltpu.VMEM((R, cap2, sub, EDGE), F32),
            pltpu.VMEM((R * cap2, sub, EDGE), F32),
            pltpu.VMEM((C, cap3, sub, EDGE), F32),
            pltpu.VMEM((C, EDGE, EDGE), F32),
            dma((C,)), dma((C,)), dma((R * C,)), dma((C, R)),
            dma((C,)), dma((C,)), dma((R,)), dma((R,)), dma((C,)), dma((C,)),
        ],
        compiler_params=pltpu.CompilerParams(
            collective_id=0, has_side_effects=True, vmem_limit_bytes=40 << 20
        ),
        name="spread",
    )(placed, index2, index3, front)


def slab_kernel(C, landing, grid, arrived, out, tile, sem):
    out[...] = grid[:, 0]
    slots = arrived.shape[1]

    def run(k):
        @pl.when(landing[1 + slots + k] == 0)
        def _():
            copy = pltpu.make_async_copy(arrived.at[:, k], tile, sem)
            copy.start()
            copy.wait()
            jl = landing[1 + k]
            out[jl] = out[jl] + tile[...].reshape(EDGE, EDGE)

    @pl.when(landing[0] < 2)
    def _():
        over(0, slots, run)


def slab_of(C, landing, grid, arrived):
    return pl.pallas_call(
        functools.partial(slab_kernel, C),
        grid=(1,),
        in_specs=[
            pl.BlockSpec(memory_space=pltpu.SMEM),
            pl.BlockSpec((C, 1, EDGE, EDGE), lambda t: (0, 0, 0, 0)),
            pl.BlockSpec(memory_space=pltpu.HBM),
        ],
        out_specs=pl.BlockSpec((C, EDGE, EDGE), lambda t: (0, 0, 0)),
        out_shape=jax.ShapeDtypeStruct((C, EDGE, EDGE), F32),
        scratch_shapes=[pltpu.VMEM((arrived.shape[0], EDGE // C, EDGE), F32), pltpu.SemaphoreType.DMA],
        name="slab",
    )(landing, grid, arrived)


STEP = 8


def factor(work, upper):
    rows8 = lax.broadcasted_iota(jnp.int32, (STEP, 1), 0)
    lanes = lax.broadcasted_iota(jnp.int32, (STEP, EDGE), 1)

    def block(b, _):
        first = pl.multiple_of(b * STEP, STEP)
        x = work[pl.ds(first, STEP), :]
        d = pltpu.roll(x[:, :EDGE], lax.rem(EDGE - first, EDGE), 1)
        for t in range(STEP):
            pivot = d[t : t + 1, t : t + 1]
            scale = lax.rsqrt(pivot)
            ratio = d[:, t : t + 1] / pivot
            ratio = jnp.where(rows8 > t, ratio, jnp.where(rows8 == t, 1.0 - scale, 0.0))
            x = x - ratio * x[t : t + 1, :]
            d = d - ratio * d[t : t + 1, :]
        upper[pl.ds(first, STEP), :] = x
        left = jnp.where(lanes >= first + STEP, x[:, :EDGE], 0.0)
        work[...] = work[...] - dot(left, x, TN)
        return 0

    lax.fori_loop(0, EDGE // STEP, block, 0)


def panel_kernel(
    R, C, slab, qrow, qcol,
    diag, rawrow, zbuf, rawcol, work, upper, low,
    dr_send, dr_recv, dx_send, dx_recv, dy_send, dy_recv, sc_send, ck_recv,
    ag_send, ag_recv, z_send, z_recv, v_send, v_recv, q_sem,
):
    r = lax.axis_index("row")
    c = lax.axis_index("col")
    X = math.isqrt(C)
    x, y = lax.rem(c, X), c // X
    ratio = C // R
    greet(R, C, r, c)

    owners = ((0, 0, 0), (1, 0, 1), (1, 1, 2))
    lines = ((0, 0, 2), (1, 2, 1))

    def diag_row(k, p):
        rr, cc, at = owners[p]
        return remote(slab.at[0], diag.at[at], dr_send.at[k], dr_recv.at[at], lax.rem(r + k, R), c)

    def diag_own(p):
        return pltpu.make_async_copy(slab.at[0], diag.at[owners[p][2]], dr_recv.at[owners[p][2]])

    for p in range(3):

        @pl.when((r == owners[p][0]) & (c == owners[p][1]))
        def _():
            for k in range(1, R):
                diag_row(k, p).start()
            diag_own(p).start()

    def scatter(jl, k):
        return remote(slab.at[jl], rawrow.at[k, jl], sc_send.at[jl], ck_recv.at[k], r, jl)

    def scatter_own(jl, k):
        return pltpu.make_async_copy(slab.at[jl], rawrow.at[k, jl], ck_recv.at[k])

    for k in range(2):

        @pl.when(c == k)
        def _():
            for jl in range(C):
                if jl == k:
                    scatter_own(jl, k).start()
                else:
                    scatter(jl, k).start()

    def diag_x(k, p):
        _, at, n = lines[p]
        here = diag.at[pl.ds(at, n)]
        return remote(here, here, dx_send.at[k], dx_recv.at[p], r, lax.rem(x + k, X))

    for p in range(2):
        owner, at, n = lines[p]

        @pl.when(c == owner)
        def _():
            for u in range(n):
                diag_own(at + u).wait()
            for k in range(1, X):
                diag_x(k, p).start()

    def diag_y(k):
        return remote(diag, diag, dy_send.at[k], dy_recv.at[0], r, k * X + x)

    @pl.when(y == 0)
    def _():
        for p in range(2):

            @pl.when(c != lines[p][0])
            def _():
                _, at, n = lines[p]
                here = diag.at[pl.ds(at, n)]
                remote(here, here, dx_send.at[0], dx_recv.at[p], r, c).wait_recv()

        for k in range(1, X):
            diag_y(k).start()

    for k in range(2):
        pltpu.make_async_copy(slab.at[0], rawrow.at[k, c], ck_recv.at[k]).wait()

    def gather(k, n):
        here = rawrow.at[n, c]
        return remote(here, here, ag_send.at[n, k], ag_recv.at[n, c], r, lax.rem(c + k, C))

    def along(k, n):
        return remote(
            rawrow.at[n, c], zbuf.at[n, r], z_send.at[n, k], z_recv.at[n, r], lax.rem(r + k, R), c
        )

    for k in range(1, R):
        for n in range(2):
            along(k, n).start()
    for k in range(1, C):
        for n in range(2):
            gather(k, n).start()

    mine = lax.rem(c, ratio) * R
    place = c // ratio

    def serve(p, n):
        return remote(
            zbuf.at[n, p], rawcol.at[n, place], v_send.at[n, p], v_recv.at[n, place], r, mine + p
        )

    def serve_own(p, n):
        return pltpu.make_async_copy(zbuf.at[n, p], rawcol.at[n, place], v_recv.at[n, place])

    own_z = [pltpu.make_async_copy(rawrow.at[n, c], zbuf.at[n, r], z_recv.at[n, r]) for n in range(2)]
    for copy in own_z:
        copy.start()
    for copy in own_z:
        copy.wait()

    def pass_on(p):
        for n in range(2):

            @pl.when(p != r)
            def _():
                remote(rawrow.at[n, 0], zbuf.at[n, p], z_send.at[n, 0], z_recv.at[n, p], r, c).wait_recv()

            @pl.when(mine + p == c)
            def _():
                serve_own(p, n).start()

            @pl.when(mine + p != c)
            def _():
                serve(p, n).start()

    over(0, R, pass_on)

    @pl.when(y != 0)
    def _():
        remote(diag, diag, dy_send.at[0], dy_recv.at[0], r, c).wait_recv()

    rows = lax.broadcasted_iota(jnp.int32, (EDGE, EDGE), 0)
    cols = lax.broadcasted_iota(jnp.int32, (EDGE, EDGE), 1)
    eye = (rows == cols).astype(F32)

    def pivot(block, at):
        work[:, :EDGE] = jnp.where(rows >= cols, block, block.T)
        work[:, EDGE:] = eye
        factor(work, upper)
        low[at] = jnp.where(rows >= cols, upper[:, :EDGE].T, 0.0)
        low[at + 1] = jnp.where(rows >= cols, upper[:, EDGE:], 0.0)

    pivot(diag[0], 0)
    low[2] = dot(diag[1], low[1], NT)
    pivot(diag[2] - dot(low[2], low[2], NT), 3)

    def solve(raw, at, count):
        a0 = raw[0, pl.ds(at, count)].reshape(count * EDGE, EDGE)
        a1 = raw[1, pl.ds(at, count)].reshape(count * EDGE, EDGE)
        q0 = dot(a0, low[1], NT)
        q1 = dot(a1 - dot(q0, low[2], NT), low[4], NT)
        raw[0, pl.ds(at, count)] = q0.reshape(count, EDGE, EDGE)
        raw[1, pl.ds(at, count)] = q1.reshape(count, EDGE, EDGE)

    def col_wait(s):
        for n in range(2):
            pltpu.make_async_copy(zbuf.at[n, 0], rawcol.at[n, s], v_recv.at[n, s]).wait()

    over(0, R, col_wait)
    many = min(4, R)
    over(0, R // many, lambda g: solve(rawcol, g * many, many))
    keep_col = pltpu.make_async_copy(rawcol, qcol, q_sem.at[0])
    keep_col.start()

    def row_wait(jl):
        @pl.when(jl != c)
        def _():
            for n in range(2):
                here = rawrow.at[n, jl]
                remote(here, here, ag_send.at[n, 0], ag_recv.at[n, jl], r, c).wait_recv()

    over(0, C, row_wait)
    for k in range(1, C):
        for n in range(2):
            gather(k, n).wait_send()
    for k in range(1, R):
        for n in range(2):
            along(k, n).wait_send()

    over(0, C // many, lambda g: solve(rawrow, g * many, many))

    @pl.when(r == 0)
    def _():
        rawrow[0, 0] = low[0]
        rawrow[1, 0] = jnp.zeros((EDGE, EDGE), F32)

    @pl.when(r == 1)
    def _():
        rawrow[0, 0] = low[2]
        rawrow[1, 0] = low[3]

    keep_row = pltpu.make_async_copy(rawrow, qrow, q_sem.at[1])
    keep_row.start()

    for p in range(3):

        @pl.when((r == owners[p][0]) & (c == owners[p][1]))
        def _():
            for k in range(1, R):
                diag_row(k, p).wait_send()

    for k in range(2):

        @pl.when(c == k)
        def _():
            for jl in range(C):
                if jl != k:
                    scatter(jl, k).wait_send()

            for s in range(1, X):
                diag_x(s, k).wait_send()

    @pl.when(y == 0)
    def _():
        for k in range(1, X):
            diag_y(k).wait_send()

    def served(p):
        @pl.when(mine + p != c)
        def _():
            for n in range(2):
                serve(p, n).wait_send()

    over(0, R, served)
    keep_col.wait()
    keep_row.wait()


def panels(R, C, slab):
    hbm = pl.BlockSpec(memory_space=pltpu.HBM)
    dma = pltpu.SemaphoreType.DMA
    X = math.isqrt(C)
    return pl.pallas_call(
        functools.partial(panel_kernel, R, C),
        in_specs=[hbm],
        out_specs=[hbm, hbm],
        out_shape=[
            jax.ShapeDtypeStruct((2, C, EDGE, EDGE), F32),
            jax.ShapeDtypeStruct((2, R, EDGE, EDGE), F32),
        ],
        scratch_shapes=[
            pltpu.VMEM((3, EDGE, EDGE), F32),
            pltpu.VMEM((2, C, EDGE, EDGE), F32),
            pltpu.VMEM((2, R, EDGE, EDGE), F32),
            pltpu.VMEM((2, R, EDGE, EDGE), F32),
            pltpu.VMEM((EDGE, 2 * EDGE), F32),
            pltpu.VMEM((EDGE, 2 * EDGE), F32),
            pltpu.VMEM((5, EDGE, EDGE), F32),
            dma((R,)), dma((3,)), dma((X,)), dma((2,)), dma((X,)), dma((1,)), dma((C,)), dma((2,)),
            dma((2, C)), dma((2, C)), dma((2, R)), dma((2, R)), dma((2, R)), dma((2, R)), dma((2,)),
        ],
        compiler_params=pltpu.CompilerParams(
            collective_id=1, has_side_effects=True, vmem_limit_bytes=40 << 20
        ),
        name="panels",
    )(slab)


def halves(x):
    high = x.astype(BF16)
    return high, (x - high.astype(F32)).astype(BF16)


def update_kernel(R, C, place, landing, grid, qrow, qcol, arrived, out, wide, head, follow):
    jl = pl.program_id(0)
    slots = arrived.shape[1]
    r, c = place[0], place[1]
    i = jl * R + r
    rows = lax.broadcasted_iota(jnp.int32, (EDGE, EDGE), 0)
    cols = lax.broadcasted_iota(jnp.int32, (EDGE, EDGE), 1)

    @pl.when(jl == 0)
    def _():
        def clear(k):
            head[k] = -1

        over(0, C, clear)

        def link(k):
            @pl.when(landing[1 + slots + k] >= 0)
            def _():
                where = landing[1 + k]
                follow[k] = head[where]
                head[where] = k

        over(0, slots, link)

        def split(s):
            for n in range(2):
                high, low = halves(qcol[n, s])
                for m, part in ((0, high), (2, low), (4, high)):
                    wide[s, :, (m + n) * EDGE : (m + n + 1) * EDGE] = part

        over(0, R, split)

    first, second = halves(qrow[0, 0]), halves(qrow[1, 0])
    left = jnp.concatenate([first[0], second[0], first[0], second[0], first[1], second[1]], axis=1)
    for s in range(R):
        j = s * C + c

        @pl.when(i < j)
        def _():
            out[0, s] = jnp.zeros((EDGE, EDGE), F32)

        @pl.when((i >= j) & (j < 2))
        def _():
            out[0, s] = jnp.where(j == 0, qrow[0, 0], qrow[1, 0])

        @pl.when((i >= j) & (j >= 2))
        def _():
            out[0, s] = grid[0, s] - dot16(left, wide[s], NT)

    def more(k):
        return k >= 0

    def add(k):
        s = landing[1 + slots + k]

        @pl.when(s * C + c >= 2)
        def _():
            out[0, s] = out[0, s] + arrived[:, k].reshape(EDGE, EDGE)

        return follow[k]

    lax.while_loop(more, add, head[jl])
    for s in range(R):

        @pl.when((i == s * C + c) & (i >= 2))
        def _():
            out[0, s] = jnp.where(rows >= cols, out[0, s], 0.0)


def update(R, C, place, landing, grid, qrow, qcol, arrived):
    cap3 = arrived.shape[1]
    block = pl.BlockSpec((1, R, EDGE, EDGE), lambda jl, *_: (jl, 0, 0, 0))
    return pl.pallas_call(
        functools.partial(update_kernel, R, C),
        grid_spec=pltpu.PrefetchScalarGridSpec(
            num_scalar_prefetch=2,
            grid=(C,),
            in_specs=[
                block,
                pl.BlockSpec((2, 1, EDGE, EDGE), lambda jl, *_: (0, jl, 0, 0)),
                pl.BlockSpec((2, R, EDGE, EDGE), lambda jl, *_: (0, 0, 0, 0)),
                pl.BlockSpec(
                    arrived.shape, lambda jl, *_: (0, 0, 0, 0),
                    pipeline_mode=pl.Buffered(1),
                ),
            ],
            out_specs=block,
            scratch_shapes=[
                pltpu.VMEM((R, EDGE, 6 * EDGE), BF16),
                pltpu.SMEM((C,), jnp.int32),
                pltpu.SMEM((cap3,), jnp.int32),
            ],
        ),
        out_shape=jax.ShapeDtypeStruct((C, R, EDGE, EDGE), F32),
        compiler_params=pltpu.CompilerParams(vmem_limit_bytes=40 << 20),
        name="update",
    )(place, landing, grid, qrow, qcol, arrived)


def capacities(R, C, T):
    if T < 32:
        return 8, 8
    return 104, 112


def hot(values, count):
    return (values[..., None] == jnp.arange(count, dtype=jnp.int32)).astype(BF16)


def before(marks):
    n = marks.shape[-2]
    serial = jnp.arange(n, dtype=jnp.int32)
    lower = (serial[:, None] > serial[None, :]).astype(BF16)
    return jnp.einsum("pq,...qk->...pk", lower, marks, preferred_element_type=F32)


def local(front_entries, child_updates, row_maps, col_maps, target_columns, row_offsets):
    R = lax.axis_size("row")
    C = lax.axis_size("col")
    count = R * C
    T = child_updates.shape[0]
    cap2, cap3 = capacities(R, C, T)
    my_row = lax.axis_index("row").astype(jnp.int32)
    my_col = lax.axis_index("col").astype(jnp.int32)

    told = jnp.concatenate([target_columns[:, 0], row_offsets[:, 0]])
    told = lax.all_to_all(
        jnp.broadcast_to(told, (count, 2 * T)), ("row", "col"), split_axis=0, concat_axis=0, tiled=True
    )
    columns, offsets = told[:, :T], told[:, T:]
    target_rows = columns + offsets % (count - columns)
    columns = columns.reshape(R, C * T)
    target_rows = target_rows.reshape(R, C * T)
    to_row, to_col = target_rows % R, columns % C

    row_hot = hot(to_row, R)
    rank2 = jnp.sum(before(row_hot) * row_hot.astype(F32), axis=-1).astype(jnp.int32)
    mine = to_row == my_row
    col_hot = hot(jnp.where(mine, to_col, -1), C)
    inside = before(col_hot)
    totals = jnp.sum(col_hot.astype(F32), axis=1)
    planes = jnp.arange(R, dtype=jnp.int32)
    ahead = jnp.sum(jnp.where((planes[:, None] > planes[None, :])[..., None], totals[None], 0.0), axis=1)
    rank3 = jnp.sum((inside + ahead[:, None, :]) * col_hot.astype(F32), axis=-1).astype(jnp.int32)
    loads2 = jnp.sum(row_hot.astype(F32), axis=1)
    loads3 = jnp.einsum("pqk,pql->kl", row_hot, hot(to_col, C), preferred_element_type=F32)
    passes2 = (jnp.max(loads2).astype(jnp.int32) + cap2 - 1) // cap2
    passes3 = (jnp.max(loads3).astype(jnp.int32) + cap3 - 1) // cap3

    def tables(a, b):
        own_hot = lax.dynamic_index_in_dim(row_hot, my_row, 0, keepdims=False)
        own_rank = lax.dynamic_index_in_dim(rank2, my_row, 0, keepdims=False)
        serial = jnp.arange(C * T, dtype=jnp.int32)
        values = jnp.stack([serial // T, serial % T], axis=0).astype(BF16)
        marked = values[:, :, None] * own_hot[None]
        found = jnp.einsum("vqk,qn->vkn", marked, hot(own_rank - a * cap2, cap2), preferred_element_type=F32)
        found = found.astype(jnp.int32)
        index2 = (found[0] * T + found[1]).reshape(-1)
        place2 = rank2 - a * cap2
        active = (place2 >= 0) & (place2 < cap2) & mine
        source = jnp.broadcast_to(planes[:, None], (R, C * T))
        values = jnp.stack(
            [source, place2, target_rows // R, columns // C, jnp.ones_like(source)], axis=0
        )
        values = jnp.where(active, values, 0).astype(BF16)
        marked = values[..., None] * col_hot[None]
        found = jnp.einsum(
            "vpqk,pqn->vkn", marked, hot(rank3 - b * cap3, cap3), preferred_element_type=F32
        ).astype(jnp.int32)
        index3 = (found[0] * cap2 + found[1]).reshape(-1)
        here = lax.dynamic_index_in_dim(found, my_col, 1, keepdims=False)
        return index2, index3, here[2], here[3], here[4]

    index2, index3, land_row, land_col, valid = tables(0, 0)
    placed = place_tiles(C, child_updates, row_maps, col_maps)
    grid, arrived = spread(
        R, C, cap2, cap3, placed, index2, index3, front_entries.reshape(count, EDGE, EDGE)
    )

    def another(carry):
        p, grid = carry
        index2, index3, land_row, land_col, valid = tables(p // passes3, p % passes3)
        held = lax.all_to_all(placed, "col", split_axis=0, concat_axis=0, tiled=True)
        held = held.reshape((C * T, EDGE // C, EDGE))[index2].reshape(R, cap2, EDGE // C, EDGE)
        held = lax.all_to_all(held, "row", split_axis=0, concat_axis=0, tiled=True)
        held = held.reshape((R * cap2, EDGE // C, EDGE))[index3].reshape(C, cap3, EDGE // C, EDGE)
        held = lax.all_to_all(held, "col", split_axis=0, concat_axis=0, tiled=True)
        tiles = held.transpose(1, 0, 2, 3).reshape(cap3, EDGE, EDGE)
        tiles = jnp.where((valid > 0)[:, None, None], tiles, 0.0)
        return p + 1, grid.at[land_row, land_col].add(tiles)

    _, grid = lax.while_loop(lambda carry: carry[0] < passes2 * passes3, another, (jnp.int32(1), grid))

    landing = jnp.concatenate([my_col[None], land_row, jnp.where(valid > 0, land_col, -1)])
    slab = slab_of(C, landing, grid, arrived)
    qrow, qcol = panels(R, C, slab)
    place = jnp.stack([my_row, my_col])
    result = update(R, C, place, landing, grid, qrow, qcol, arrived)
    return result.reshape(C, 1, R, 1, EDGE, EDGE)


def solution(mesh):
    return jax.shard_map(
        local,
        mesh=mesh,
        in_specs=(
            P(None, ("row", "col")),
            P(("row", "col"), None, None),
            P(("row", "col"), None),
            P(("row", "col"), None),
            P(("row", "col"), None),
            P(("row", "col"), None),
        ),
        out_specs=P(None, "row", None, "col", None, None),
        check_vma=False,
    )
```

time: 979 us -> 367 us (0.37)
  waiting for transfers between devices: 746 us -> 0.01 us
  Pallas kernels: 0 us -> 329 us
  other arithmetic: 119 us -> 3.26 us
  local copies, waits for them, and re-layouts: 39.8 us -> 8.54 us
  matrix products: 28.1 us -> 2.01 us
  starting transfers between devices: 31.2 us -> 17.6 us
  between operations: 13.9 us -> 1.63 us
    psum x6 -> x0, waiting for transfers between devices: 411 us -> none  [broadcast(): return lax.psum(kept, axis)]
    all_to_all x3 -> x2, waiting for transfers between devices: 335 us -> 0.01 us  [the longest x1 0.01 us: local(): lax.all_to_all(jnp.broadcast_to(told, (count, 2 * T)), ('row', 'col'), sp...]
    pallas_call x0 -> x5, Pallas kernels: none -> 329 us  [the longest x1 183 us: spread(): pl.pallas_call(functools.partial(spread_kernel, R, C, cap2, cap3), in_spe...]
    scatter-add x1 -> x0, other arithmetic: 55 us -> none  [local(): jax.ops.segment_sum(arrived, landing, num_segments=block_count)]
    another operation x10 -> x3, other arithmetic: 45.8 us -> 0.1 us  [the longest x1 0.08 us: local(): place = jnp.stack([my_row, my_col])]
    dot_general x4 -> x5, matrix products: 24.6 us -> 2.01 us  [the longest x1 0.77 us: local(): jnp.einsum('pqk,pql->kl', row_hot, hot(to_col, C), preferred_element_type...]
    all_to_all x3 -> x2, starting transfers between devices: 30.3 us -> 17.6 us  [the longest x1 10.4 us: local(): lax.all_to_all(jnp.broadcast_to(told, (count, 2 * T)), ('row', 'col'), sp...]
  transfers between devices with their start and end apart: 9 -> 2, of which waited for: 8 -> 0; matrix products, arithmetic and copies ran while one was open for 2% -> 0% of each run, Pallas kernels for 0% -> 53%
where the time goes in v2:
time: 367 us; the launch traced here: 362 us
  Pallas kernels  329 us (90%)
  starting transfers between devices  17.6 us (5%)
  local copies, waits for them, and re-layouts  8.54 us (2%)
    pallas_call x1, Pallas kernels, spread(): pl.pallas_call(functools.partial(spread_kernel, R, C, cap2, cap3), in_spe...  183 us
    pallas_call x1, Pallas kernels, panels(): pl.pallas_call(functools.partial(panel_kernel, R, C), in_specs=[hbm], out...  110 us
    pallas_call x1, Pallas kernels, update(): pl.pallas_call(functools.partial(update_kernel, R, C), grid_spec=pltpu.Pr...  23.1 us
    all_to_all x1, starting transfers between devices, local(): lax.all_to_all(jnp.broadcast_to(told, (count, 2 * T)), ('row', 'col'), sp...  10.4 us
    pallas_call x1, Pallas kernels, place_tiles(): pl.pallas_call(functools.partial(place_kernel, C), grid=(count // GROUP,)...  9.55 us
    unnamed x11, local copies, waits for them, and re-layouts  7.35 us
  transfers between devices with their start and end apart: 2, of which 0 were waited for; matrix products, arithmetic and copies ran while one was open for 0% of the time, Pallas kernels for 53%

profile of v2, /device:TPU:12, one launch (start us, length us, event | category | flops | bytes accessed | tf_op | source)
XLA Modules:
  0.0 362.1 jit_solution(9048335966165680208)
XLA Ops:
  0.0 0.7 pad_add_fusion.2
  0.8 0.7 broadcast_in_dim.68
  1.5 10.4 %all-to-all-start.2 = ((s32[128,1,64]{2,1,0:T(1,128)}), s32[128,1,64]{2,1,0:T(1,128)S(1)}, u32[]{:S(2)}, u32[]{:S(2)}) async-start(s32[128,1,64]{2,1,0:T(1,128)} %broadcast_in_dim.68), calls=%async_computation.2 | async-start | bytes 131072 | tf_op jit(solution)/shard_map/all_to_all | solution.py:721
  11.9 0.1 pad_add_fusion.1.place
  11.9 9.5 %place.1.placed = f32[16,32,8,128]{3,2,1,0:T(8,128)} custom-call(f32[32,128,128]{2,1,0:T(8,128)} %tile.1, s32[32,128]{1,0:T(8,128)} %row_map.1, s32[32,128]{1,0:T(8,128)} %col_map.1), custom_call_target="tpu_custom_call" | custom-call | tf_op jit(solution)/shard_map/place/pallas_call | solution.py:78
  21.5 0.8 fusion.88
  22.3 0.1 reshape.869
  22.3 0.1 reshape.870
  22.4 0.1 convert_reduce_fusion.1
  22.5 0.6 reduce_max.18
  23.8 0.3 fusion.45
  24.1 0.1 reshape.872
  24.2 0.1 reshape.871
  24.3 0.8 fusion.57
  25.8 0.1 convert_reduce_fusion
  25.9 0.1 select_reduce_fusion
  26.0 0.3 fusion.43
  26.4 0.2 convolution_convert_fusion.1
  26.6 0.1 add.317.index2
  26.6 7.2 %all-to-all-start.3 = ((f32[16,32,8,128]{3,2,1,0:T(8,128)}), f32[16,32,8,128]{3,2,1,0:T(8,128)}, u32[]{:S(2)}, u32[]{:S(2)}) async-start(f32[16,32,8,128]{3,2,1,0:T(8,128)} %place.1.placed), calls=%async_computation.3 | async-start | bytes 4194304 | tf_op jit(solution)/shard_map/while/body/all_to_all | solution.py:777
  34.0 0.5 fusion.49
  34.5 0.1 add.319.index3
  34.6 183.5 %spread.1 = (f32[16,8,128,128]{3,2,1,0:T(8,128)}, f32[16,112,8,128]{3,2,1,0:T(8,128)S(1)}) custom-call(f32[16,32,8,128]{3,2,1,0:T(8,128)S(1)} %copy-done.2, s32[832]{0:T(1024)S(1)} %add.317.index2, s32[1792]{0:T(1024)S(1)} %add.319.index3, f32[128,128,128]{2,1,0:T(8,128)} %bitcast.152), custom_call_target="tpu_custom_call" | custom-call | tf_op jit(solution)/shard_map/spread/pallas_call | solution.py:244
  218.1 0.0 copy-start
  218.1 3.0 copy-done
  221.2 0.6 pad_add_fusion.landing
  221.8 2.4 slab.1
  224.2 1.2 copy-done.3
  225.4 110.5 %panels.1 = (f32[2,16,128,128]{3,2,1,0:T(8,128)S(1)}, f32[2,8,128,128]{3,2,1,0:T(8,128)S(1)}) custom-call(f32[16,128,128]{2,1,0:T(8,128)S(1)} %copy-done.3), custom_call_target="tpu_custom_call" | custom-call | tf_op jit(solution)/shard_map/panels/pallas_call | solution.py:564
  335.9 0.0 copy-start.1
  335.9 3.1 copy-done.1
  339.0 23.1 %update.1 = f32[16,8,128,128]{3,2,1,0:T(8,128)} custom-call(s32[2]{0:T(128)S(1)} %pad_add_fusion.1.place, s32[225]{0:T(256)S(1)} %copy-done.4, f32[16,8,128,128]{3,2,1,0:T(8,128)} %get-tuple-element.347.grid, f32[2,16,128,128]{3,2,1,0:T(8,128)S(1)} %get-tuple-element.349.qrow, f32[2,8,128,128]{3,2,1,0:T(8,128)S(1)} %get-tuple-element.350.qcol, ...), custom_call_target="tpu_custom_call" | custom-call | tf_op jit(solution)/shard_map/update/pallas_call | solution.py:667
  (30 shorter events, 0.2 us)
Async XLA Ops:
  1.5 20.0 %all-to-all-start.2 = ((s32[128,1,64]{2,1,0:T(1,128)}), s32[128,1,64]{2,1,0:T(1,128)S(1)}, u32[]{:S(2)}, u32[]{:S(2)}) async-start(s32[128,1,64]{2,1,0:T(1,128)} %broadcast_in_dim.68), calls=%async_computation.2 | async-start | bytes 131072 | tf_op jit(solution)/shard_map/all_to_all | solution.py:721
  21.5 13.1 %copy-start.2 = (f32[16,32,8,128]{3,2,1,0:T(8,128)S(1)}, f32[16,32,8,128]{3,2,1,0:T(8,128)}, u32[]{:S(2)}) copy-start(f32[16,32,8,128]{3,2,1,0:T(8,128)} %place.1.placed) | copy-start | bytes 6291460
  26.6 195.1 %all-to-all-start.3 = ((f32[16,32,8,128]{3,2,1,0:T(8,128)}), f32[16,32,8,128]{3,2,1,0:T(8,128)}, u32[]{:S(2)}, u32[]{:S(2)}) async-start(f32[16,32,8,128]{3,2,1,0:T(8,128)} %place.1.placed), calls=%async_computation.3 | async-start | bytes 4194304 | tf_op jit(solution)/shard_map/while/body/all_to_all | solution.py:777
  218.1 3.1 copy-start
  221.8 114.1 %copy-start.4 = (s32[225]{0:T(256)S(1)}, s32[225]{0:T(256)}, u32[]{:S(2)}) copy-start(s32[225]{0:T(256)} %pad_add_fusion.landing) | copy-start | bytes 2704
  224.2 1.2 copy-start.3
  335.9 3.1 copy-start.1

commit v3 on v2

--- a/solution.py
+++ b/solution.py
@@ -85,6 +85,10 @@
     )(tiles, row_map, col_map)
 
 
+PARTS = 4
+PACK = 4
+
+
 def spread_kernel(
     R, C, cap2, cap3, placed, index2, index3, col, grid, out,
     r1, s2, r2, s3, stage,
@@ -98,18 +102,27 @@
     i0 = start_of(r * C + c)
     greet(R, C, r, c)
 
-    def first(k):
+    part1 = T // PARTS
+
+    def first(k, h):
         to = lax.rem(c + k, C)
-        return remote(placed.at[to], r1.at[pl.ds(c * T, T)], p1_send.at[k], p1_recv.at[c], r, to)
-
-    def first_wait(k):
+        return remote(
+            placed.at[to, pl.ds(h * part1, part1)], r1.at[pl.ds(c * T + h * part1, part1)],
+            p1_send.at[k, h], p1_recv.at[c, h], r, to,
+        )
+
+    def first_wait(k, h):
         src = lax.rem(c + k, C)
-        remote(placed.at[0], r1.at[pl.ds(src * T, T)], p1_send.at[0], p1_recv.at[src], r, c).wait_recv()
-
-    first_own = pltpu.make_async_copy(placed.at[c], r1.at[pl.ds(c * T, T)], p1_recv.at[c])
+        remote(
+            placed.at[0, pl.ds(0, part1)], r1.at[pl.ds(src * T + h * part1, part1)],
+            p1_send.at[0, h], p1_recv.at[src, h], r, c,
+        ).wait_recv()
+
+    first_own = pltpu.make_async_copy(placed.at[c], r1.at[pl.ds(c * T, T)], p1_recv.at[c, 0])
     first_own.start()
-    for k in range(1, C):
-        first(k).start()
+    for h in range(PARTS):
+        for k in range(1, C):
+            first(k, h).start()
 
     def b_copy(i):
         return remote(
@@ -149,8 +162,9 @@
     own_blocks(own_turn)
 
     first_own.wait()
-    for k in range(1, C):
-        first_wait(k)
+    for h in range(PARTS):
+        for k in range(1, C):
+            first_wait(k, h)
 
     def second(k):
         to = lax.rem(r + k, R)
@@ -160,16 +174,14 @@
         src = lax.rem(r + k, R)
         remote(s2.at[0], r2.at[pl.ds(src * cap2, cap2)], p2_send.at[0], p2_recv.at[src], r, c).wait_recv()
 
-    UNROLL = 8
-
     def pack2(k):
         to = lax.rem(r + k, R)
 
         def run(n):
-            for u in range(UNROLL):
-                s2[to, n * UNROLL + u] = r1[index2[to * cap2 + n * UNROLL + u]]
-
-        over(0, cap2 // UNROLL, run)
+            for u in range(PACK):
+                s2[to, n * PACK + u] = r1[index2[to * cap2 + n * PACK + u]]
+
+        over(0, cap2 // PACK, run)
 
     for k in range(1, R):
         pack2(k)
@@ -177,41 +189,53 @@
             second(k - 1).start()
 
     def pack2_own(n):
-        for u in range(UNROLL):
-            r2[r * cap2 + n * UNROLL + u] = r1[index2[r * cap2 + n * UNROLL + u]]
-
-    over(0, cap2 // UNROLL, pack2_own)
+        for u in range(PACK):
+            r2[r * cap2 + n * PACK + u] = r1[index2[r * cap2 + n * PACK + u]]
+
+    over(0, cap2 // PACK, pack2_own)
     second(R - 1).start()
     sent_blocks(middle, NB, lambda i: b_copy(i).start())
 
     for k in range(1, R):
         second_wait(k)
 
-    def third(k):
+    part3 = cap3 // PARTS
+
+    def third(k, h):
         to = lax.rem(c + k, C)
-        return remote(s3.at[to], out.at[c], p3_send.at[k], p3_recv.at[c], r, to)
-
-    def third_wait(k):
+        at = pl.ds(h * part3, part3)
+        return remote(s3.at[to, at], out.at[c, at], p3_send.at[k, h], p3_recv.at[c, h], r, to)
+
+    def third_wait(k, h):
         src = lax.rem(c + k, C)
-        remote(s3.at[0], out.at[src], p3_send.at[0], p3_recv.at[src], r, c).wait_recv()
-
-    third_own = pltpu.make_async_copy(s3.at[c], out.at[c], p3_recv.at[c])
-
-    def pack3(k):
+        at = pl.ds(h * part3, part3)
+        remote(s3.at[0, at], out.at[src, at], p3_send.at[0, h], p3_recv.at[src, h], r, c).wait_recv()
+
+    third_own = pltpu.make_async_copy(s3.at[c], out.at[c], p3_recv.at[c, 0])
+
+    def pack3(k, h):
         to = lax.rem(c + k, C)
 
         def run(n):
-            for u in range(UNROLL):
-                s3[to, n * UNROLL + u] = r2[index3[to * cap3 + n * UNROLL + u]]
-
-        over(0, cap3 // UNROLL, run)
-
-    for k in range(1, C):
-        pack3(k)
-        if k > 1:
-            third(k - 1).start()
-    pack3(C)
-    third(C - 1).start()
+            for u in range(PACK):
+                at = h * part3 + n * PACK + u
+                s3[to, at] = r2[index3[to * cap3 + at]]
+
+        over(0, part3 // PACK, run)
+
+    def third_part(h):
+        def step(k):
+            pack3(k, h)
+
+            @pl.when(k > 1)
+            def _():
+                third(k - 1, h).start()
+
+        over(1, C, step)
+        pack3(C, h)
+        third(C - 1, h).start()
+
+    over(0, PARTS, third_part)
 
     own_blocks(lambda jl: own_out(jl).wait())
     for s in range(R):
@@ -225,14 +249,16 @@
         over(0, C, run)
     third_own.start()
     sent_blocks(i0, NB, lambda i: b_copy(i).wait_send())
-    for k in range(1, C):
-        first(k).wait_send()
+    for h in range(PARTS):
+        for k in range(1, C):
+            first(k, h).wait_send()
     for k in range(1, R):
         second(k).wait_send()
-    for k in range(1, C):
-        third_wait(k)
-    for k in range(1, C):
-        third(k).wait_send()
+    for h in range(PARTS):
+        for k in range(1, C):
+            third_wait(k, h)
+        for k in range(1, C):
+            third(k, h).wait_send()
     third_own.wait()
 
 
@@ -256,10 +282,10 @@
             pltpu.VMEM((C, cap3, sub, EDGE), F32),
             pltpu.VMEM((C, EDGE, EDGE), F32),
             dma((C,)), dma((C,)), dma((R * C,)), dma((C, R)),
-            dma((C,)), dma((C,)), dma((R,)), dma((R,)), dma((C,)), dma((C,)),
+            dma((C, PARTS)), dma((C, PARTS)), dma((R,)), dma((R,)), dma((C, PARTS)), dma((C, PARTS)),
         ],
         compiler_params=pltpu.CompilerParams(
-            collective_id=0, has_side_effects=True, vmem_limit_bytes=40 << 20
+            collective_id=0, has_side_effects=True, vmem_limit_bytes=60 << 20
         ),
         name="spread",
     )(placed, index2, index3, front)
@@ -295,6 +321,7 @@
         out_specs=pl.BlockSpec((C, EDGE, EDGE), lambda t: (0, 0, 0)),
         out_shape=jax.ShapeDtypeStruct((C, EDGE, EDGE), F32),
         scratch_shapes=[pltpu.VMEM((arrived.shape[0], EDGE // C, EDGE), F32), pltpu.SemaphoreType.DMA],
+        compiler_params=pltpu.CompilerParams(vmem_limit_bytes=60 << 20),
         name="slab",
     )(landing, grid, arrived)
 
@@ -403,6 +430,10 @@
         for k in range(1, X):
             diag_y(k).start()
 
+    @pl.when(y != 0)
+    def _():
+        remote(diag, diag, dy_send.at[0], dy_recv.at[0], r, c).wait_recv()
+
     for k in range(2):
         pltpu.make_async_copy(slab.at[0], rawrow.at[k, c], ck_recv.at[k]).wait()
 
@@ -418,8 +449,8 @@
     for k in range(1, R):
         for n in range(2):
             along(k, n).start()
-    for k in range(1, C):
-        for n in range(2):
+    for n in range(2):
+        for k in range(1, C):
             gather(k, n).start()
 
     mine = lax.rem(c, ratio) * R
@@ -436,8 +467,6 @@
     own_z = [pltpu.make_async_copy(rawrow.at[n, c], zbuf.at[n, r], z_recv.at[n, r]) for n in range(2)]
     for copy in own_z:
         copy.start()
-    for copy in own_z:
-        copy.wait()
 
     def pass_on(p):
         for n in range(2):
@@ -453,12 +482,6 @@
             @pl.when(mine + p != c)
             def _():
                 serve(p, n).start()
-
-    over(0, R, pass_on)
-
-    @pl.when(y != 0)
-    def _():
-        remote(diag, diag, dy_send.at[0], dy_recv.at[0], r, c).wait_recv()
 
     rows = lax.broadcasted_iota(jnp.int32, (EDGE, EDGE), 0)
     cols = lax.broadcasted_iota(jnp.int32, (EDGE, EDGE), 1)
@@ -472,6 +495,9 @@
         low[at + 1] = jnp.where(rows >= cols, upper[:, EDGE:], 0.0)
 
     pivot(diag[0], 0)
+    for copy in own_z:
+        copy.wait()
+    over(0, R, pass_on)
     low[2] = dot(diag[1], low[1], NT)
     pivot(diag[2] - dot(low[2], low[2], NT), 3)
 
@@ -581,7 +607,7 @@
             dma((2, C)), dma((2, C)), dma((2, R)), dma((2, R)), dma((2, R)), dma((2, R)), dma((2,)),
         ],
         compiler_params=pltpu.CompilerParams(
-            collective_id=1, has_side_effects=True, vmem_limit_bytes=40 << 20
+            collective_id=1, has_side_effects=True, vmem_limit_bytes=60 << 20
         ),
         name="panels",
     )(slab)
@@ -619,8 +645,9 @@
         def split(s):
             for n in range(2):
                 high, low = halves(qcol[n, s])
-                for m, part in ((0, high), (2, low), (4, high)):
-                    wide[s, :, (m + n) * EDGE : (m + n + 1) * EDGE] = part
+                at = pl.ds(pl.multiple_of(s * EDGE, EDGE), EDGE)
+                for m, part in ((0, high.T), (2, low.T), (4, high.T)):
+                    wide[(m + n) * EDGE : (m + n + 1) * EDGE, at] = part
 
         over(0, R, split)
 
@@ -639,7 +666,7 @@
 
         @pl.when((i >= j) & (j >= 2))
         def _():
-            out[0, s] = grid[0, s] - dot16(left, wide[s], NT)
+            out[0, s] = grid[0, s] - dot16(left, wide[:, s * EDGE : (s + 1) * EDGE], NN)
 
     def more(k):
         return k >= 0
@@ -680,20 +707,20 @@
             ],
             out_specs=block,
             scratch_shapes=[
-                pltpu.VMEM((R, EDGE, 6 * EDGE), BF16),
+                pltpu.VMEM((6 * EDGE, R * EDGE), BF16),
                 pltpu.SMEM((C,), jnp.int32),
                 pltpu.SMEM((cap3,), jnp.int32),
             ],
         ),
         out_shape=jax.ShapeDtypeStruct((C, R, EDGE, EDGE), F32),
-        compiler_params=pltpu.CompilerParams(vmem_limit_bytes=40 << 20),
+        compiler_params=pltpu.CompilerParams(vmem_limit_bytes=60 << 20),
         name="update",
     )(place, landing, grid, qrow, qcol, arrived)
 
 
 def capacities(R, C, T):
     if T < 32:
-        return 8, 8
+        return 8, 16
     return 104, 112
 
 
@@ -773,8 +800,9 @@
 
     def another(carry):
         p, grid = carry
+        p, tiles = lax.optimization_barrier((p, placed))
         index2, index3, land_row, land_col, valid = tables(p // passes3, p % passes3)
-        held = lax.all_to_all(placed, "col", split_axis=0, concat_axis=0, tiled=True)
+        held = lax.all_to_all(tiles, "col", split_axis=0, concat_axis=0, tiled=True)
         held = held.reshape((C * T, EDGE // C, EDGE))[index2].reshape(R, cap2, EDGE // C, EDGE)
         held = lax.all_to_all(held, "row", split_axis=0, concat_axis=0, tiled=True)
         held = held.reshape((R * cap2, EDGE // C, EDGE))[index3].reshape(C, cap3, EDGE // C, EDGE)

time: 367 us -> 349 us (0.951)
  starting transfers between devices: 17.6 us -> 10.4 us
  local copies, waits for them, and re-layouts: 8.54 us -> 2.4 us
    pallas_call x1, Pallas kernels: 183 us -> 151 us  [spread(): pl.pallas_call(functools.partial(spread_kernel, R, C, cap2, cap3), in_spe...]
    pallas_call x1, Pallas kernels: 110 us -> 136 us  [panels(): pl.pallas_call(functools.partial(panel_kernel, R, C), in_specs=[hbm], out...]
    unnamed x11 -> x1, local copies, waits for them, and re-layouts: 7.35 us -> 0.01 us
    all_to_all x1 -> x0, starting transfers between devices: 7.25 us -> none  [another(): lax.all_to_all(placed, 'col', split_axis=0, concat_axis=0, tiled=True)]
    pallas_call x1, Pallas kernels: 23.1 us -> 27.2 us  [update(): pl.pallas_call(functools.partial(update_kernel, R, C), grid_spec=pltpu.Pr...]
  transfers between devices with their start and end apart: 2 -> 1, of which waited for: 0 -> 0; matrix products, arithmetic and copies ran while one was open for 0% -> 0% of each run, Pallas kernels for 53% -> 3%
where the time goes in v3:
time: 349 us; the launch traced here: 347 us
  Pallas kernels  326 us (93%)
  starting transfers between devices  10.4 us (3%)
  other arithmetic  4.48 us (1%)
    pallas_call x1, Pallas kernels, spread(): pl.pallas_call(functools.partial(spread_kernel, R, C, cap2, cap3), in_spe...  151 us
    pallas_call x1, Pallas kernels, panels(): pl.pallas_call(functools.partial(panel_kernel, R, C), in_specs=[hbm], out...  136 us
    pallas_call x1, Pallas kernels, update(): pl.pallas_call(functools.partial(update_kernel, R, C), grid_spec=pltpu.Pr...  27.2 us
    all_to_all x1, starting transfers between devices, local(): lax.all_to_all(jnp.broadcast_to(told, (count, 2 * T)), ('row', 'col'), sp...  10.4 us
    pallas_call x1, Pallas kernels, place_tiles(): pl.pallas_call(functools.partial(place_kernel, C), grid=(count // GROUP,)...  9.54 us
  transfers between devices with their start and end apart: 1, of which 0 were waited for; matrix products, arithmetic and copies ran while one was open for 0% of the time, Pallas kernels for 3%

profile of v3, /device:TPU:12, one launch (start us, length us, event | category | flops | bytes accessed | tf_op | source)
XLA Modules:
  0.0 346.7 jit_solution(9701555603520006157)
XLA Ops:
  0.0 0.7 pad_add_fusion.2
  0.8 0.7 broadcast_in_dim.68
  1.5 10.4 %all-to-all-start.3 = ((s32[128,1,64]{2,1,0:T(1,128)}), s32[128,1,64]{2,1,0:T(1,128)S(1)}, u32[]{:S(2)}, u32[]{:S(2)}) async-start(s32[128,1,64]{2,1,0:T(1,128)} %broadcast_in_dim.68), calls=%async_computation.3 | async-start | bytes 131072 | tf_op jit(solution)/shard_map/all_to_all | solution.py:748
  11.9 0.6 pad_add_fusion.1.place
  12.5 9.5 %place.1.placed = f32[16,32,8,128]{3,2,1,0:T(8,128)} custom-call(f32[32,128,128]{2,1,0:T(8,128)} %tile.1, s32[32,128]{1,0:T(8,128)} %row_map.1, s32[32,128]{1,0:T(8,128)} %col_map.1), custom_call_target="tpu_custom_call" | custom-call | tf_op jit(solution)/shard_map/place/pallas_call | solution.py:78
  22.0 0.0 all-to-all-done.3
  22.0 0.8 fusion.88
  22.8 0.1 reshape.869
  22.9 0.1 reshape.870
  23.0 0.1 convert_reduce_fusion.1
  23.1 0.6 reduce_max.18
  24.4 0.3 fusion.45
  24.7 0.1 reshape.872
  24.8 0.1 reshape.871
  24.9 0.8 fusion.57
  26.4 0.1 convert_reduce_fusion
  26.6 0.1 select_reduce_fusion
  26.7 0.3 fusion.43
  27.0 0.2 convolution_convert_fusion.1
  27.2 0.7 add.317.index2
  27.9 0.6 fusion.89
  28.5 0.5 fusion.49
  29.0 0.7 add.319.index3
  29.7 0.6 pad_add_fusion.landing
  30.4 150.6 %spread.1 = (f32[16,8,128,128]{3,2,1,0:T(8,128)}, f32[16,112,8,128]{3,2,1,0:T(8,128)}) custom-call(f32[16,32,8,128]{3,2,1,0:T(8,128)} %place.1.placed, s32[832]{0:T(1024)} %add.317.index2, s32[1792]{0:T(1024)} %add.319.index3, f32[128,128,128]{2,1,0:T(8,128)} %bitcast.155), custom_call_target="tpu_custom_call" | custom-call | tf_op jit(solution)/shard_map/spread/pallas_call | solution.py:270
  181.0 2.3 slab.1
  183.3 136.2 %panels.1 = (f32[2,16,128,128]{3,2,1,0:T(8,128)}, f32[2,8,128,128]{3,2,1,0:T(8,128)}) custom-call(f32[16,128,128]{2,1,0:T(8,128)} %slab.1), custom_call_target="tpu_custom_call" | custom-call | tf_op jit(solution)/shard_map/panels/pallas_call | solution.py:590
  319.5 27.2 %update.1 = f32[16,8,128,128]{3,2,1,0:T(8,128)} custom-call(s32[2]{0:T(128)} %pad_add_fusion.1.place, s32[225]{0:T(256)} %pad_add_fusion.landing, f32[16,8,128,128]{3,2,1,0:T(8,128)} %get-tuple-element.345.grid, f32[2,16,128,128]{3,2,1,0:T(8,128)} %get-tuple-element.347.qrow, f32[2,8,128,128]{3,2,1,0:T(8,128)} %get-tuple-element.348.qcol, ...), custom_call_target="tpu_custom_call" | custom-call | tf_op jit(solution)/shard_map/update/pallas_call | solution.py:694
  (22 shorter events, 0.2 us)
Async XLA Ops:
  1.5 20.6 %all-to-all-start.3 = ((s32[128,1,64]{2,1,0:T(1,128)}), s32[128,1,64]{2,1,0:T(1,128)S(1)}, u32[]{:S(2)}, u32[]{:S(2)}) async-start(s32[128,1,64]{2,1,0:T(1,128)} %broadcast_in_dim.68), calls=%async_computation.3 | async-start | bytes 131072 | tf_op jit(solution)/shard_map/all_to_all | solution.py:748

commit v4 on v3

--- a/solution.py
+++ b/solution.py
@@ -85,13 +85,40 @@
     )(tiles, row_map, col_map)
 
 
+STEP = 8
+
+
+def factor(work, upper):
+    rows8 = lax.broadcasted_iota(jnp.int32, (STEP, 1), 0)
+    lanes = lax.broadcasted_iota(jnp.int32, (STEP, EDGE), 1)
+
+    def block(b, _):
+        first = pl.multiple_of(b * STEP, STEP)
+        x = work[pl.ds(first, STEP), :]
+        d = pltpu.roll(x[:, :EDGE], lax.rem(EDGE - first, EDGE), 1)
+        for t in range(STEP):
+            pivot = d[t : t + 1, t : t + 1]
+            scale = lax.rsqrt(pivot)
+            ratio = d[:, t : t + 1] / pivot
+            ratio = jnp.where(rows8 > t, ratio, jnp.where(rows8 == t, 1.0 - scale, 0.0))
+            x = x - ratio * x[t : t + 1, :]
+            d = d - ratio * d[t : t + 1, :]
+        upper[pl.ds(first, STEP), :] = x
+        left = jnp.where(lanes >= first + STEP, x[:, :EDGE], 0.0)
+        work[...] = work[...] - dot(left, x, TN)
+        return 0
+
+    lax.fori_loop(0, EDGE // STEP, block, 0)
+
+
 PARTS = 4
 PACK = 4
 
 
 def spread_kernel(
-    R, C, cap2, cap3, placed, index2, index3, col, grid, out,
-    r1, s2, r2, s3, stage,
+    R, C, cap2, cap3, placed, index2, index3, pick, col, grid, out, low_out,
+    r1, s2, r2, s3, stage, diag, mine, parts, work, upper, low,
+    dr_send, dr_recv, dx_send, dx_recv, dy_send, dy_recv, m_send, m_recv, g_send, g_recv, low_sem,
     st_in, st_out, b_send, b_recv, p1_send, p1_recv, p2_send, p2_recv, p3_send, p3_recv,
 ):
     r = lax.axis_index("row")
@@ -100,7 +127,37 @@
     T = placed.shape[1]
     start_of = lambda column: jnp.where(column < 2, 0, column)
     i0 = start_of(r * C + c)
+    X = math.isqrt(C)
+    x, y = lax.rem(c, X), c // X
     greet(R, C, r, c)
+
+    pieces = ((0, 0, 2), (1, 2, 1))
+
+    def diag_row(p, k):
+        owner, at, n = pieces[p]
+        return remote(
+            col.at[pl.ds(owner, n)], diag.at[pl.ds(at, n)], dr_send.at[k], dr_recv.at[p], lax.rem(r + k, R), c
+        )
+
+    def diag_own(p):
+        owner, at, n = pieces[p]
+        return pltpu.make_async_copy(col.at[pl.ds(owner, n)], diag.at[pl.ds(at, n)], dr_recv.at[p])
+
+    def diag_x(p, k):
+        _, at, n = pieces[p]
+        here = diag.at[pl.ds(at, n)]
+        return remote(here, here, dx_send.at[k], dx_recv.at[p], r, lax.rem(x + k, X))
+
+    def diag_y(k):
+        return remote(diag, diag, dy_send.at[k], dy_recv.at[0], r, k * X + x)
+
+    for p in range(2):
+
+        @pl.when((r == 0) & (c == pieces[p][0]))
+        def _():
+            for k in range(1, R):
+                diag_row(p, k).start()
+            diag_own(p).start()
 
     part1 = T // PARTS
 
@@ -151,7 +208,7 @@
 
         over(low, high, run)
 
-    middle = i0 + (NB - i0) // 4
+    middle = i0 + (NB - i0) // 3
     own_blocks(lambda jl: own_in(jl).start())
     sent_blocks(i0, middle, lambda i: b_copy(i).start())
 
@@ -166,6 +223,14 @@
         for k in range(1, C):
             first_wait(k, h)
 
+    for p in range(2):
+
+        @pl.when(c == pieces[p][0])
+        def _():
+            diag_own(p).wait()
+            for k in range(1, X):
+                diag_x(p, k).start()
+
     def second(k):
         to = lax.rem(r + k, R)
         return remote(s2.at[to], r2.at[pl.ds(r * cap2, cap2)], p2_send.at[k], p2_recv.at[r], to, c)
@@ -194,10 +259,70 @@
 
     over(0, cap2 // PACK, pack2_own)
     second(R - 1).start()
-    sent_blocks(middle, NB, lambda i: b_copy(i).start())
+
+    @pl.when(y == 0)
+    def _():
+        for p in range(2):
+
+            @pl.when(c != pieces[p][0])
+            def _():
+                _, at, n = pieces[p]
+                here = diag.at[pl.ds(at, n)]
+                remote(here, here, dx_send.at[0], dx_recv.at[p], r, c).wait_recv()
+
+        for k in range(1, X):
+            diag_y(k).start()
 
     for k in range(1, R):
         second_wait(k)
+
+    owned = ((0, 1), (1, 2))
+
+    def mine_own_rows(p):
+        at, n = owned[p]
+        return mine.at[pl.ds(at, n)]
+
+    def mine_row(p, k):
+        here = mine_own_rows(p)
+        return remote(here, here, m_send.at[k], m_recv.at[p], lax.rem(r + k, R), c)
+
+    for p in range(2):
+
+        @pl.when(r == p)
+        def _():
+            at, n = owned[p]
+            zero = jnp.zeros(mine.shape[1:], F32)
+
+            def run(k, sums):
+                for u in range(PACK):
+                    slot = k * PACK + u
+                    sums = tuple(
+                        total + pick[b * R * cap2 + slot] * r2[slot] for b, total in enumerate(sums)
+                    )
+                return sums
+
+            sums = lax.fori_loop(0, R * cap2 // PACK, run, (zero,) * n)
+            for b in range(n):
+                mine[at + b] = sums[b]
+            for k in range(1, R):
+                mine_row(p, k).start()
+
+    for p in range(2):
+
+        @pl.when(r != p)
+        def _():
+            here = mine_own_rows(p)
+            remote(here, here, m_send.at[0], m_recv.at[p], r, c).wait_recv()
+
+    def mine_col(k):
+        to = lax.rem(c + k, C)
+        return remote(mine, parts.at[c], g_send.at[k], g_recv.at[c], r, to)
+
+    for k in range(1, C):
+        mine_col(k).start()
+    parts[c] = mine[...]
+    sent_blocks(middle, NB, lambda i: b_copy(i).start())
+
 
     part3 = cap3 // PARTS
 
@@ -236,6 +361,52 @@
         third(C - 1, h).start()
 
     over(0, PARTS, third_part)
+
+    @pl.when(y != 0)
+    def _():
+        remote(diag, diag, dy_send.at[0], dy_recv.at[0], r, c).wait_recv()
+
+    sub = mine.shape[1]
+
+    def part_wait(q):
+        @pl.when(q != c)
+        def _():
+            remote(mine, parts.at[q], g_send.at[0], g_recv.at[q], r, c).wait_recv()
+
+    over(0, C, part_wait)
+    for k in range(1, X):
+
+        @pl.when(y == 0)
+        def _():
+            diag_y(k).wait_send()
+
+    for p in range(2):
+
+        @pl.when(c == pieces[p][0])
+        def _():
+            for k in range(1, X):
+                diag_x(p, k).wait_send()
+
+    rows = lax.broadcasted_iota(jnp.int32, (EDGE, EDGE), 0)
+    cols = lax.broadcasted_iota(jnp.int32, (EDGE, EDGE), 1)
+    eye = (rows == cols).astype(F32)
+    for q in range(C):
+        for b in range(3):
+            at = pl.ds(q * sub, sub)
+            diag[b, at, :] = diag[b, at, :] + parts[q, b]
+
+    def pivot(block, at):
+        work[:, :EDGE] = jnp.where(rows >= cols, block, block.T)
+        work[:, EDGE:] = eye
+        factor(work, upper)
+        low[at] = jnp.where(rows >= cols, upper[:, :EDGE].T, 0.0)
+        low[at + 1] = jnp.where(rows >= cols, upper[:, EDGE:], 0.0)
+
+    pivot(diag[0], 0)
+    low[2] = dot(diag[1], low[1], NT)
+    pivot(diag[2] - dot(low[2], low[2], NT), 3)
+    low_copy = pltpu.make_async_copy(low, low_out, low_sem)
+    low_copy.start()
 
     own_blocks(lambda jl: own_out(jl).wait())
     for s in range(R):
@@ -260,20 +431,36 @@
         for k in range(1, C):
             third(k, h).wait_send()
     third_own.wait()
-
-
-def spread(R, C, cap2, cap3, placed, index2, index3, front):
+    low_copy.wait()
+    for p in range(2):
+
+        @pl.when((r == 0) & (c == pieces[p][0]))
+        def _():
+            for k in range(1, R):
+                diag_row(p, k).wait_send()
+
+        @pl.when(r == p)
+        def _():
+            for k in range(1, R):
+                mine_row(p, k).wait_send()
+
+    for k in range(1, C):
+        mine_col(k).wait_send()
+
+
+def spread(R, C, cap2, cap3, placed, index2, index3, pick, front):
     hbm = pl.BlockSpec(memory_space=pltpu.HBM)
     smem = pl.BlockSpec(memory_space=pltpu.SMEM)
     dma = pltpu.SemaphoreType.DMA
     T, sub = placed.shape[1], placed.shape[2]
     return pl.pallas_call(
         functools.partial(spread_kernel, R, C, cap2, cap3),
-        in_specs=[hbm, smem, smem, hbm],
-        out_specs=[hbm, hbm],
+        in_specs=[hbm, smem, smem, smem, hbm],
+        out_specs=[hbm, hbm, hbm],
         out_shape=[
             jax.ShapeDtypeStruct((C, R, EDGE, EDGE), F32),
             jax.ShapeDtypeStruct((C, cap3, sub, EDGE), F32),
+            jax.ShapeDtypeStruct((5, EDGE, EDGE), F32),
         ],
         scratch_shapes=[
             pltpu.VMEM((C * T, sub, EDGE), F32),
@@ -281,6 +468,14 @@
             pltpu.VMEM((R * cap2, sub, EDGE), F32),
             pltpu.VMEM((C, cap3, sub, EDGE), F32),
             pltpu.VMEM((C, EDGE, EDGE), F32),
+            pltpu.VMEM((3, EDGE, EDGE), F32),
+            pltpu.VMEM((3, sub, EDGE), F32),
+            pltpu.VMEM((C, 3, sub, EDGE), F32),
+            pltpu.VMEM((EDGE, 2 * EDGE), F32),
+            pltpu.VMEM((EDGE, 2 * EDGE), F32),
+            pltpu.VMEM((5, EDGE, EDGE), F32),
+            dma((R,)), dma((2,)), dma((C,)), dma((2,)), dma((C,)), dma((1,)),
+            dma((R,)), dma((2,)), dma((C,)), dma((C,)), dma,
             dma((C,)), dma((C,)), dma((R * C,)), dma((C, R)),
             dma((C, PARTS)), dma((C, PARTS)), dma((R,)), dma((R,)), dma((C, PARTS)), dma((C, PARTS)),
         ],
@@ -288,7 +483,7 @@
             collective_id=0, has_side_effects=True, vmem_limit_bytes=60 << 20
         ),
         name="spread",
-    )(placed, index2, index3, front)
+    )(placed, index2, index3, pick, front)
 
 
 def slab_kernel(C, landing, grid, arrived, out, tile, sem):
@@ -326,68 +521,21 @@
     )(landing, grid, arrived)
 
 
-STEP = 8
-
-
-def factor(work, upper):
-    rows8 = lax.broadcasted_iota(jnp.int32, (STEP, 1), 0)
-    lanes = lax.broadcasted_iota(jnp.int32, (STEP, EDGE), 1)
-
-    def block(b, _):
-        first = pl.multiple_of(b * STEP, STEP)
-        x = work[pl.ds(first, STEP), :]
-        d = pltpu.roll(x[:, :EDGE], lax.rem(EDGE - first, EDGE), 1)
-        for t in range(STEP):
-            pivot = d[t : t + 1, t : t + 1]
-            scale = lax.rsqrt(pivot)
-            ratio = d[:, t : t + 1] / pivot
-            ratio = jnp.where(rows8 > t, ratio, jnp.where(rows8 == t, 1.0 - scale, 0.0))
-            x = x - ratio * x[t : t + 1, :]
-            d = d - ratio * d[t : t + 1, :]
-        upper[pl.ds(first, STEP), :] = x
-        left = jnp.where(lanes >= first + STEP, x[:, :EDGE], 0.0)
-        work[...] = work[...] - dot(left, x, TN)
-        return 0
-
-    lax.fori_loop(0, EDGE // STEP, block, 0)
-
-
 def panel_kernel(
-    R, C, slab, qrow, qcol,
-    diag, rawrow, zbuf, rawcol, work, upper, low,
-    dr_send, dr_recv, dx_send, dx_recv, dy_send, dy_recv, sc_send, ck_recv,
-    ag_send, ag_recv, z_send, z_recv, v_send, v_recv, q_sem,
+    R, C, slab, low, qrow, qcol,
+    chunk, rows_q, zbuf, cols_q,
+    sc_send, ck_recv, ag_send, ag_recv, z_send, z_recv, v_send, v_recv, q_sem,
 ):
     r = lax.axis_index("row")
     c = lax.axis_index("col")
-    X = math.isqrt(C)
-    x, y = lax.rem(c, X), c // X
     ratio = C // R
     greet(R, C, r, c)
 
-    owners = ((0, 0, 0), (1, 0, 1), (1, 1, 2))
-    lines = ((0, 0, 2), (1, 2, 1))
-
-    def diag_row(k, p):
-        rr, cc, at = owners[p]
-        return remote(slab.at[0], diag.at[at], dr_send.at[k], dr_recv.at[at], lax.rem(r + k, R), c)
-
-    def diag_own(p):
-        return pltpu.make_async_copy(slab.at[0], diag.at[owners[p][2]], dr_recv.at[owners[p][2]])
-
-    for p in range(3):
-
-        @pl.when((r == owners[p][0]) & (c == owners[p][1]))
-        def _():
-            for k in range(1, R):
-                diag_row(k, p).start()
-            diag_own(p).start()
-
     def scatter(jl, k):
-        return remote(slab.at[jl], rawrow.at[k, jl], sc_send.at[jl], ck_recv.at[k], r, jl)
+        return remote(slab.at[jl], chunk.at[k], sc_send.at[jl], ck_recv.at[k], r, jl)
 
     def scatter_own(jl, k):
-        return pltpu.make_async_copy(slab.at[jl], rawrow.at[k, jl], ck_recv.at[k])
+        return pltpu.make_async_copy(slab.at[jl], chunk.at[k], ck_recv.at[k])
 
     for k in range(2):
 
@@ -399,55 +547,25 @@
                 else:
                     scatter(jl, k).start()
 
-    def diag_x(k, p):
-        _, at, n = lines[p]
-        here = diag.at[pl.ds(at, n)]
-        return remote(here, here, dx_send.at[k], dx_recv.at[p], r, lax.rem(x + k, X))
-
-    for p in range(2):
-        owner, at, n = lines[p]
-
-        @pl.when(c == owner)
-        def _():
-            for u in range(n):
-                diag_own(at + u).wait()
-            for k in range(1, X):
-                diag_x(k, p).start()
-
-    def diag_y(k):
-        return remote(diag, diag, dy_send.at[k], dy_recv.at[0], r, k * X + x)
-
-    @pl.when(y == 0)
-    def _():
-        for p in range(2):
-
-            @pl.when(c != lines[p][0])
-            def _():
-                _, at, n = lines[p]
-                here = diag.at[pl.ds(at, n)]
-                remote(here, here, dx_send.at[0], dx_recv.at[p], r, c).wait_recv()
-
-        for k in range(1, X):
-            diag_y(k).start()
-
-    @pl.when(y != 0)
-    def _():
-        remote(diag, diag, dy_send.at[0], dy_recv.at[0], r, c).wait_recv()
-
-    for k in range(2):
-        pltpu.make_async_copy(slab.at[0], rawrow.at[k, c], ck_recv.at[k]).wait()
+    i = c * R + r
+    scatter_own(0, 0).wait()
+    q0 = dot(chunk[0], low[1], NT)
+    scatter_own(0, 1).wait()
+    q1 = dot(chunk[1] - dot(q0, low[2], NT), low[4], NT)
+    rows_q[0, c] = jnp.where(i == 0, low[0], jnp.where(i == 1, low[2], q0))
+    rows_q[1, c] = jnp.where(i == 0, 0.0, jnp.where(i == 1, low[3], q1))
 
     def gather(k, n):
-        here = rawrow.at[n, c]
+        here = rows_q.at[n, c]
         return remote(here, here, ag_send.at[n, k], ag_recv.at[n, c], r, lax.rem(c + k, C))
 
     def along(k, n):
         return remote(
-            rawrow.at[n, c], zbuf.at[n, r], z_send.at[n, k], z_recv.at[n, r], lax.rem(r + k, R), c
+            rows_q.at[n, c], zbuf.at[n, r], z_send.at[n, k], z_recv.at[n, r], lax.rem(r + k, R), c
         )
 
-    for k in range(1, R):
-        for n in range(2):
+    for n in range(2):
+        for k in range(1, R):
             along(k, n).start()
     for n in range(2):
         for k in range(1, C):
@@ -458,22 +576,24 @@
 
     def serve(p, n):
         return remote(
-            zbuf.at[n, p], rawcol.at[n, place], v_send.at[n, p], v_recv.at[n, place], r, mine + p
+            zbuf.at[n, p], cols_q.at[n, place], v_send.at[n, p], v_recv.at[n, place], r, mine + p
         )
 
     def serve_own(p, n):
-        return pltpu.make_async_copy(zbuf.at[n, p], rawcol.at[n, place], v_recv.at[n, place])
-
-    own_z = [pltpu.make_async_copy(rawrow.at[n, c], zbuf.at[n, r], z_recv.at[n, r]) for n in range(2)]
+        return pltpu.make_async_copy(zbuf.at[n, p], cols_q.at[n, place], v_recv.at[n, place])
+
+    own_z = [pltpu.make_async_copy(rows_q.at[n, c], zbuf.at[n, r], z_recv.at[n, r]) for n in range(2)]
     for copy in own_z:
         copy.start()
+    for copy in own_z:
+        copy.wait()
 
     def pass_on(p):
         for n in range(2):
 
             @pl.when(p != r)
             def _():
-                remote(rawrow.at[n, 0], zbuf.at[n, p], z_send.at[n, 0], z_recv.at[n, p], r, c).wait_recv()
+                remote(rows_q.at[n, 0], zbuf.at[n, p], z_send.at[n, 0], z_recv.at[n, p], r, c).wait_recv()
 
             @pl.when(mine + p == c)
             def _():
@@ -483,78 +603,26 @@
             def _():
                 serve(p, n).start()
 
-    rows = lax.broadcasted_iota(jnp.int32, (EDGE, EDGE), 0)
-    cols = lax.broadcasted_iota(jnp.int32, (EDGE, EDGE), 1)
-    eye = (rows == cols).astype(F32)
-
-    def pivot(block, at):
-        work[:, :EDGE] = jnp.where(rows >= cols, block, block.T)
-        work[:, EDGE:] = eye
-        factor(work, upper)
-        low[at] = jnp.where(rows >= cols, upper[:, :EDGE].T, 0.0)
-        low[at + 1] = jnp.where(rows >= cols, upper[:, EDGE:], 0.0)
-
-    pivot(diag[0], 0)
-    for copy in own_z:
-        copy.wait()
     over(0, R, pass_on)
-    low[2] = dot(diag[1], low[1], NT)
-    pivot(diag[2] - dot(low[2], low[2], NT), 3)
-
-    def solve(raw, at, count):
-        a0 = raw[0, pl.ds(at, count)].reshape(count * EDGE, EDGE)
-        a1 = raw[1, pl.ds(at, count)].reshape(count * EDGE, EDGE)
-        q0 = dot(a0, low[1], NT)
-        q1 = dot(a1 - dot(q0, low[2], NT), low[4], NT)
-        raw[0, pl.ds(at, count)] = q0.reshape(count, EDGE, EDGE)
-        raw[1, pl.ds(at, count)] = q1.reshape(count, EDGE, EDGE)
+
+    def row_wait(jl):
+        @pl.when(jl != c)
+        def _():
+            for n in range(2):
+                here = rows_q.at[n, jl]
+                remote(here, here, ag_send.at[n, 0], ag_recv.at[n, jl], r, c).wait_recv()
+
+    over(0, C, row_wait)
+    keep_row = pltpu.make_async_copy(rows_q, qrow, q_sem.at[1])
+    keep_row.start()
 
     def col_wait(s):
         for n in range(2):
-            pltpu.make_async_copy(zbuf.at[n, 0], rawcol.at[n, s], v_recv.at[n, s]).wait()
+            pltpu.make_async_copy(zbuf.at[n, 0], cols_q.at[n, s], v_recv.at[n, s]).wait()
 
     over(0, R, col_wait)
-    many = min(4, R)
-    over(0, R // many, lambda g: solve(rawcol, g * many, many))
-    keep_col = pltpu.make_async_copy(rawcol, qcol, q_sem.at[0])
+    keep_col = pltpu.make_async_copy(cols_q, qcol, q_sem.at[0])
     keep_col.start()
-
-    def row_wait(jl):
-        @pl.when(jl != c)
-        def _():
-            for n in range(2):
-                here = rawrow.at[n, jl]
-                remote(here, here, ag_send.at[n, 0], ag_recv.at[n, jl], r, c).wait_recv()
-
-    over(0, C, row_wait)
-    for k in range(1, C):
-        for n in range(2):
-            gather(k, n).wait_send()
-    for k in range(1, R):
-        for n in range(2):
-            along(k, n).wait_send()
-
-    over(0, C // many, lambda g: solve(rawrow, g * many, many))
-
-    @pl.when(r == 0)
-    def _():
-        rawrow[0, 0] = low[0]
-        rawrow[1, 0] = jnp.zeros((EDGE, EDGE), F32)
-
-    @pl.when(r == 1)
-    def _():
-        rawrow[0, 0] = low[2]
-        rawrow[1, 0] = low[3]
-
-    keep_row = pltpu.make_async_copy(rawrow, qrow, q_sem.at[1])
-    keep_row.start()
-
-    for p in range(3):
-
-        @pl.when((r == owners[p][0]) & (c == owners[p][1]))
-        def _():
-            for k in range(1, R):
-                diag_row(k, p).wait_send()
 
     for k in range(2):
 
@@ -564,13 +632,11 @@
                 if jl != k:
                     scatter(jl, k).wait_send()
 
-            for s in range(1, X):
-                diag_x(s, k).wait_send()
-
-    @pl.when(y == 0)
-    def _():
-        for k in range(1, X):
-            diag_y(k).wait_send()
+    for n in range(2):
+        for k in range(1, C):
+            gather(k, n).wait_send()
+        for k in range(1, R):
+            along(k, n).wait_send()
 
     def served(p):
         @pl.when(mine + p != c)
@@ -583,34 +649,30 @@
     keep_row.wait()
 
 
-def panels(R, C, slab):
+def panels(R, C, slab, low):
     hbm = pl.BlockSpec(memory_space=pltpu.HBM)
     dma = pltpu.SemaphoreType.DMA
-    X = math.isqrt(C)
     return pl.pallas_call(
         functools.partial(panel_kernel, R, C),
-        in_specs=[hbm],
+        in_specs=[hbm, pl.BlockSpec(memory_space=pltpu.VMEM)],
         out_specs=[hbm, hbm],
         out_shape=[
             jax.ShapeDtypeStruct((2, C, EDGE, EDGE), F32),
             jax.ShapeDtypeStruct((2, R, EDGE, EDGE), F32),
         ],
         scratch_shapes=[
-            pltpu.VMEM((3, EDGE, EDGE), F32),
+            pltpu.VMEM((2, EDGE, EDGE), F32),
             pltpu.VMEM((2, C, EDGE, EDGE), F32),
             pltpu.VMEM((2, R, EDGE, EDGE), F32),
             pltpu.VMEM((2, R, EDGE, EDGE), F32),
-            pltpu.VMEM((EDGE, 2 * EDGE), F32),
-            pltpu.VMEM((EDGE, 2 * EDGE), F32),
-            pltpu.VMEM((5, EDGE, EDGE), F32),
-            dma((R,)), dma((3,)), dma((X,)), dma((2,)), dma((X,)), dma((1,)), dma((C,)), dma((2,)),
-            dma((2, C)), dma((2, C)), dma((2, R)), dma((2, R)), dma((2, R)), dma((2, R)), dma((2,)),
+            dma((C,)), dma((2,)), dma((2, C)), dma((2, C)),
+            dma((2, R)), dma((2, R)), dma((2, R)), dma((2, R)), dma((2,)),
         ],
         compiler_params=pltpu.CompilerParams(
             collective_id=1, has_side_effects=True, vmem_limit_bytes=60 << 20
         ),
         name="panels",
-    )(slab)
+    )(slab, low)
 
 
 def halves(x):
@@ -618,97 +680,100 @@
     return high, (x - high.astype(F32)).astype(BF16)
 
 
-def update_kernel(R, C, place, landing, grid, qrow, qcol, arrived, out, wide, head, follow):
-    jl = pl.program_id(0)
+def update_kernel(R, C, place, landing, grid, qrow, qcol, arrived, out, left, right, head, follow):
+    s = pl.program_id(0)
     slots = arrived.shape[1]
     r, c = place[0], place[1]
-    i = jl * R + r
+    j = s * C + c
     rows = lax.broadcasted_iota(jnp.int32, (EDGE, EDGE), 0)
     cols = lax.broadcasted_iota(jnp.int32, (EDGE, EDGE), 1)
 
-    @pl.when(jl == 0)
+    @pl.when(s == 0)
     def _():
         def clear(k):
             head[k] = -1
 
-        over(0, C, clear)
+        over(0, R, clear)
 
         def link(k):
-            @pl.when(landing[1 + slots + k] >= 0)
+            where = landing[1 + slots + k]
+
+            @pl.when(where >= 0)
             def _():
-                where = landing[1 + k]
                 follow[k] = head[where]
                 head[where] = k
 
         over(0, slots, link)
 
-        def split(s):
+        def split(jl):
+            at = pl.ds(pl.multiple_of(jl * EDGE, EDGE), EDGE)
             for n in range(2):
-                high, low = halves(qcol[n, s])
-                at = pl.ds(pl.multiple_of(s * EDGE, EDGE), EDGE)
-                for m, part in ((0, high.T), (2, low.T), (4, high.T)):
-                    wide[(m + n) * EDGE : (m + n + 1) * EDGE, at] = part
-
-        over(0, R, split)
-
-    first, second = halves(qrow[0, 0]), halves(qrow[1, 0])
-    left = jnp.concatenate([first[0], second[0], first[0], second[0], first[1], second[1]], axis=1)
-    for s in range(R):
-        j = s * C + c
-
-        @pl.when(i < j)
-        def _():
-            out[0, s] = jnp.zeros((EDGE, EDGE), F32)
-
-        @pl.when((i >= j) & (j < 2))
-        def _():
-            out[0, s] = jnp.where(j == 0, qrow[0, 0], qrow[1, 0])
-
-        @pl.when((i >= j) & (j >= 2))
-        def _():
-            out[0, s] = grid[0, s] - dot16(left, wide[:, s * EDGE : (s + 1) * EDGE], NN)
+                high, low = halves(qrow[n, jl])
+                for m, part in ((0, high), (2, high), (4, low)):
+                    left[at, (m + n) * EDGE : (m + n + 1) * EDGE] = part
+
+        over(0, C, split)
+
+    for n in range(2):
+        high, low = halves(qcol[n, 0])
+        for m, part in ((0, high.T), (2, low.T), (4, high.T)):
+            right[(m + n) * EDGE : (m + n + 1) * EDGE, :] = part
+
+    many = min(4, C)
+    for g in range(C // many):
+        last = (g * many + many - 1) * R + r
+
+        @pl.when((last >= j) & (j >= 2))
+        def _():
+            product = dot16(left[g * many * EDGE : (g + 1) * many * EDGE, :], right[...], NN)
+            for u in range(many):
+                out[g * many + u, 0] = grid[g * many + u, 0] - product[u * EDGE : (u + 1) * EDGE, :]
+
+    @pl.when(j < 2)
+    def _():
+        for jl in range(C):
+            out[jl, 0] = jnp.where(j == 0, qrow[0, jl], qrow[1, jl])
 
     def more(k):
         return k >= 0
 
     def add(k):
-        s = landing[1 + slots + k]
-
-        @pl.when(s * C + c >= 2)
-        def _():
-            out[0, s] = out[0, s] + arrived[:, k].reshape(EDGE, EDGE)
-
+        jl = landing[1 + k]
+        out[jl, 0] = out[jl, 0] + arrived[:, k].reshape(EDGE, EDGE)
         return follow[k]
 
-    lax.while_loop(more, add, head[jl])
-    for s in range(R):
-
-        @pl.when((i == s * C + c) & (i >= 2))
-        def _():
-            out[0, s] = jnp.where(rows >= cols, out[0, s], 0.0)
+    lax.while_loop(more, add, jnp.where(j >= 2, head[s], -1))
+    for jl in range(C):
+        i = jl * R + r
+
+        @pl.when(i < j)
+        def _():
+            out[jl, 0] = jnp.zeros((EDGE, EDGE), F32)
+
+        @pl.when((i == j) & (j >= 2))
+        def _():
+            out[jl, 0] = jnp.where(rows >= cols, out[jl, 0], 0.0)
 
 
 def update(R, C, place, landing, grid, qrow, qcol, arrived):
     cap3 = arrived.shape[1]
-    block = pl.BlockSpec((1, R, EDGE, EDGE), lambda jl, *_: (jl, 0, 0, 0))
+    block = pl.BlockSpec((C, 1, EDGE, EDGE), lambda s, *_: (0, s, 0, 0))
     return pl.pallas_call(
         functools.partial(update_kernel, R, C),
         grid_spec=pltpu.PrefetchScalarGridSpec(
             num_scalar_prefetch=2,
-            grid=(C,),
+            grid=(R,),
             in_specs=[
                 block,
-                pl.BlockSpec((2, 1, EDGE, EDGE), lambda jl, *_: (0, jl, 0, 0)),
-                pl.BlockSpec((2, R, EDGE, EDGE), lambda jl, *_: (0, 0, 0, 0)),
-                pl.BlockSpec(
-                    arrived.shape, lambda jl, *_: (0, 0, 0, 0),
-                    pipeline_mode=pl.Buffered(1),
-                ),
+                pl.BlockSpec((2, C, EDGE, EDGE), lambda s, *_: (0, 0, 0, 0)),
+                pl.BlockSpec((2, 1, EDGE, EDGE), lambda s, *_: (0, s, 0, 0)),
+                pl.BlockSpec(arrived.shape, lambda s, *_: (0, 0, 0, 0), pipeline_mode=pl.Buffered(1)),
             ],
             out_specs=block,
             scratch_shapes=[
-                pltpu.VMEM((6 * EDGE, R * EDGE), BF16),
-                pltpu.SMEM((C,), jnp.int32),
+                pltpu.VMEM((C * EDGE, 6 * EDGE), BF16),
+                pltpu.VMEM((6 * EDGE, EDGE), BF16),
+                pltpu.SMEM((R,), jnp.int32),
                 pltpu.SMEM((cap3,), jnp.int32),
             ],
         ),
@@ -755,7 +820,12 @@
     to_row, to_col = target_rows % R, columns % C
 
     row_hot = hot(to_row, R)
-    rank2 = jnp.sum(before(row_hot) * row_hot.astype(F32), axis=-1).astype(jnp.int32)
+    pivotal = (target_rows < 2) & (columns < 2)
+    lead = row_hot * pivotal[..., None].astype(BF16)
+    rest = row_hot - lead
+    leads = jnp.sum(lead.astype(F32), axis=1, keepdims=True)
+    rank2 = before(lead) * lead.astype(F32) + (before(rest) + leads) * rest.astype(F32)
+    rank2 = jnp.sum(rank2, axis=-1).astype(jnp.int32)
     mine = to_row == my_row
     col_hot = hot(jnp.where(mine, to_col, -1), C)
     inside = before(col_hot)
@@ -793,9 +863,11 @@
         return index2, index3, here[2], here[3], here[4]
 
     index2, index3, land_row, land_col, valid = tables(0, 0)
+    marks = jnp.stack([mine & pivotal & (columns == k) & (rank2 < cap2) for k in range(2)])
+    pick = jnp.einsum("vpq,pqn->vpn", marks.astype(BF16), hot(rank2, cap2), preferred_element_type=F32)
     placed = place_tiles(C, child_updates, row_maps, col_maps)
-    grid, arrived = spread(
-        R, C, cap2, cap3, placed, index2, index3, front_entries.reshape(count, EDGE, EDGE)
+    grid, arrived, low = spread(
+        R, C, cap2, cap3, placed, index2, index3, pick.reshape(-1), front_entries.reshape(count, EDGE, EDGE)
     )
 
     def another(carry):
@@ -815,7 +887,7 @@
 
     landing = jnp.concatenate([my_col[None], land_row, jnp.where(valid > 0, land_col, -1)])
     slab = slab_of(C, landing, grid, arrived)
-    qrow, qcol = panels(R, C, slab)
+    qrow, qcol = panels(R, C, slab, low)
     place = jnp.stack([my_row, my_col])
     result = update(R, C, place, landing, grid, qrow, qcol, arrived)
     return result.reshape(C, 1, R, 1, EDGE, EDGE)

time: 349 us -> 300 us (0.86)
  Pallas kernels: 326 us -> 276 us
    pallas_call x1, Pallas kernels: 136 us -> 74.6 us  [panels(): pl.pallas_call(functools.partial(panel_kernel, R, C), in_specs=[hbm, pl.B...]
    pallas_call x1, Pallas kernels: 151 us -> 171 us  [spread(): pl.pallas_call(functools.partial(spread_kernel, R, C, cap2, cap3), in_spe...]
    pallas_call x1, Pallas kernels: 27.2 us -> 17.9 us  [update(): pl.pallas_call(functools.partial(update_kernel, R, C), grid_spec=pltpu.Pr...]
where the time goes in v4:
time: 300 us; the launch traced here: 298 us
  Pallas kernels  276 us (92%)
  starting transfers between devices  10.4 us (3%)
  other arithmetic  3.92 us (1%)
  local copies, waits for them, and re-layouts  3.09 us (1%)
    pallas_call x1, Pallas kernels, spread(): pl.pallas_call(functools.partial(spread_kernel, R, C, cap2, cap3), in_spe...  171 us
    pallas_call x1, Pallas kernels, panels(): pl.pallas_call(functools.partial(panel_kernel, R, C), in_specs=[hbm, pl.B...  74.6 us
    pallas_call x1, Pallas kernels, update(): pl.pallas_call(functools.partial(update_kernel, R, C), grid_spec=pltpu.Pr...  17.9 us
    all_to_all x1, starting transfers between devices, local(): lax.all_to_all(jnp.broadcast_to(told, (count, 2 * T)), ('row', 'col'), sp...  10.4 us
    pallas_call x1, Pallas kernels, place_tiles(): pl.pallas_call(functools.partial(place_kernel, C), grid=(count // GROUP,)...  9.54 us
  transfers between devices with their start and end apart: 1, of which 0 were waited for; matrix products, arithmetic and copies ran while one was open for 0% of the time, Pallas kernels for 3%

profile of v4, /device:TPU:12, one launch (start us, length us, event | category | flops | bytes accessed | tf_op | source)
XLA Modules:
  0.0 297.6 jit_solution(2291821724428064673)
XLA Ops:
  0.0 0.7 pad_add_fusion.3
  0.8 0.7 broadcast_in_dim.68
  1.5 10.4 %all-to-all-start.3 = ((s32[128,1,64]{2,1,0:T(1,128)}), s32[128,1,64]{2,1,0:T(1,128)S(1)}, u32[]{:S(2)}, u32[]{:S(2)}) async-start(s32[128,1,64]{2,1,0:T(1,128)} %broadcast_in_dim.68), calls=%async_computation.3 | async-start | bytes 131072 | tf_op jit(solution)/shard_map/all_to_all | solution.py:813
  11.9 0.6 pad_add_fusion.2.place
  12.5 9.5 %place.1.placed = f32[16,32,8,128]{3,2,1,0:T(8,128)} custom-call(f32[32,128,128]{2,1,0:T(8,128)} %tile.1, s32[32,128]{1,0:T(8,128)} %row_map.1, s32[32,128]{1,0:T(8,128)} %col_map.1), custom_call_target="tpu_custom_call" | custom-call | tf_op jit(solution)/shard_map/place/pallas_call | solution.py:78
  22.0 0.0 all-to-all-done.3
  22.0 0.8 fusion.110
  22.8 0.1 reshape.1007
  22.9 0.1 reshape.1009
  23.0 0.1 reshape.1008
  23.0 0.1 reshape.1010
  23.2 0.1 convert_reduce_fusion.2
  23.3 0.6 reduce_max.18
  24.6 0.3 fusion.48
  24.9 0.3 fusion.49
  25.2 0.8 fusion.64
  26.7 0.1 convert_reduce_fusion
  26.9 0.2 convolution_convert_fusion.1
  27.0 0.7 add.348.index2
  27.8 0.4 fusion.56
  28.2 0.7 reshape.1011.pick
  28.9 0.1 select_reduce_fusion
  29.0 0.3 fusion.44
  29.3 0.5 fusion.53
  29.8 0.7 add.350.index3
  30.5 0.7 pad_add_fusion.1.landing
  31.2 171.4 %spread.1 = (f32[16,8,128,128]{3,2,1,0:T(8,128)}, f32[16,112,8,128]{3,2,1,0:T(8,128)}, f32[5,128,128]{2,1,0:T(8,128)}) custom-call(f32[16,32,8,128]{3,2,1,0:T(8,128)} %place.1.placed, s32[832]{0:T(1024)} %add.348.index2, s32[1792]{0:T(1024)} %add.350.index3, f32[1664]{0:T(1024)} %reshape.1011.pick, f32[128,128,128]{2,1,0:T(8,128)} %bitcast.166), custom_call_target="tpu_custom_call" | custom-call | tf_op jit(solution)/shard_map/spread/pallas_call | solution.py:456
  202.6 0.2 while.14
  202.8 2.3 slab.1
  205.1 74.6 %panels.1 = (f32[2,16,128,128]{3,2,1,0:T(8,128)}, f32[2,8,128,128]{3,2,1,0:T(8,128)}) custom-call(f32[16,128,128]{2,1,0:T(8,128)} %slab.1, f32[5,128,128]{2,1,0:T(8,128)} %get-tuple-element.348.low), custom_call_target="tpu_custom_call" | custom-call | tf_op jit(solution)/shard_map/panels/pallas_call | solution.py:655
  279.7 17.9 %update.1 = f32[16,8,128,128]{3,2,1,0:T(8,128)} custom-call(s32[2]{0:T(128)} %pad_add_fusion.2.place, s32[225]{0:T(256)} %pad_add_fusion.1.landing, f32[16,8,128,128]{3,2,1,0:T(8,128)} %get-tuple-element.346.grid, f32[2,16,128,128]{3,2,1,0:T(8,128)} %get-tuple-element.349.qrow, f32[2,8,128,128]{3,2,1,0:T(8,128)} %get-tuple-element.350.qcol, ...), custom_call_target="tpu_custom_call" | custom-call | tf_op jit(solution)/shard_map/update/pallas_call | solution.py:761
  (27 shorter events, 0.3 us)
Async XLA Ops:
  1.5 20.6 %all-to-all-start.3 = ((s32[128,1,64]{2,1,0:T(1,128)}), s32[128,1,64]{2,1,0:T(1,128)S(1)}, u32[]{:S(2)}, u32[]{:S(2)}) async-start(s32[128,1,64]{2,1,0:T(1,128)} %broadcast_in_dim.68), calls=%async_computation.3 | async-start | bytes 131072 | tf_op jit(solution)/shard_map/all_to_all | solution.py:813

commit v5 on v4

--- a/solution.py
+++ b/solution.py
@@ -49,40 +49,125 @@
     pl.semaphore_wait(barrier, R + C - 2)
 
 
+PARTS = 4
 GROUP = 4
 
 
-def place_kernel(C, tile, row_map, col_map, out):
-    t = pl.program_id(0)
+def begin_kernel(
+    R, C, tiles, row_map, col_map, told, r1, told_all,
+    held, placed, told_row,
+    t_sem, tr_send, tr_recv, tc_send, tc_recv, send, recv,
+):
+    r = lax.axis_index("row")
+    c = lax.axis_index("col")
+    T = tiles.shape[0]
+    sub = EDGE // C
+    part = T // PARTS
+    load = pltpu.make_async_copy(tiles, held, t_sem)
+    load.start()
+    greet(R, C, r, c)
+
+    def tell_row(k):
+        return remote(told, told_row.at[r], tr_send.at[k], tr_recv.at[r], lax.rem(r + k, R), c)
+
+    def tell_col(k):
+        return remote(told_row, told_all.at[c], tc_send.at[k], tc_recv.at[c], r, lax.rem(c + k, C))
+
+    tell_own = pltpu.make_async_copy(told, told_row.at[r], tr_recv.at[r])
+    tell_own.start()
+    for k in range(1, R):
+        tell_row(k).start()
+
     levels = lax.broadcasted_iota(jnp.int32, (EDGE, EDGE), 0)
-    for g in range(GROUP):
-        k = t * GROUP + g
-        col_hot = (levels == col_map[pl.ds(k, 1), :]).astype(F32).astype(BF16)
-        row_hot = (levels == row_map[pl.ds(k, 1), :]).astype(F32).astype(BF16)
-        x = tile[g]
-        first = x.astype(BF16)
-        rest = x - first.astype(F32)
-        second = rest.astype(BF16)
-        third = (rest - second.astype(F32)).astype(BF16)
-        parts = [dot16(p, col_hot, NT).astype(BF16) for p in (first, second, third)]
-        placed = (
-            dot16(row_hot, parts[0], NN) + dot16(row_hot, parts[1], NN)
-        ) + dot16(row_hot, parts[2], NN)
-        for q in range(C):
-            out[q, g] = placed[q * (EDGE // C) : (q + 1) * (EDGE // C), :]
-
-
-def place_tiles(C, tiles, row_map, col_map):
-    count = tiles.shape[0]
-    whole = pl.BlockSpec((count, EDGE), lambda t: (0, 0))
+
+    def place(t):
+        for g in range(GROUP):
+            k = t * GROUP + g
+            col_hot = (levels == col_map[pl.ds(k, 1), :]).astype(F32).astype(BF16)
+            row_hot = (levels == row_map[pl.ds(k, 1), :]).astype(F32).astype(BF16)
+            x = held[k]
+            first = x.astype(BF16)
+            rest = x - first.astype(F32)
+            second = rest.astype(BF16)
+            third = (rest - second.astype(F32)).astype(BF16)
+            moved = [dot16(p, col_hot, NT).astype(BF16) for p in (first, second, third)]
+            full = (dot16(row_hot, moved[0], NN) + dot16(row_hot, moved[1], NN)) + dot16(
+                row_hot, moved[2], NN
+            )
+            for q in range(C):
+                placed[q, k] = full[q * sub : (q + 1) * sub, :]
+
+    def slices(k, h):
+        to = lax.rem(c + k, C)
+        return remote(
+            placed.at[to, pl.ds(h * part, part)], r1.at[pl.ds(c * T + h * part, part)],
+            send.at[k, h], recv.at[c, h], r, to,
+        )
+
+    def slices_wait(k, h):
+        src = lax.rem(c + k, C)
+        remote(
+            placed.at[0, pl.ds(0, part)], r1.at[pl.ds(src * T + h * part, part)],
+            send.at[0, h], recv.at[src, h], r, c,
+        ).wait_recv()
+
+    load.wait()
+    for h in range(PARTS):
+        over(h * part // GROUP, (h + 1) * part // GROUP, place)
+        if h == 0:
+            tell_own.wait()
+            for k in range(1, R):
+                src = lax.rem(r + k, R)
+                remote(told, told_row.at[src], tr_send.at[0], tr_recv.at[src], r, c).wait_recv()
+            for k in range(1, C):
+                tell_col(k).start()
+            tell_kept = pltpu.make_async_copy(told_row, told_all.at[c], tc_recv.at[c])
+            tell_kept.start()
+        for k in range(1, C):
+            slices(k, h).start()
+    own = pltpu.make_async_copy(placed.at[c], r1.at[pl.ds(c * T, T)], recv.at[c, 0])
+    own.start()
+    tell_kept.wait()
+    for k in range(1, C):
+        src = lax.rem(c + k, C)
+        remote(told_row, told_all.at[src], tc_send.at[0], tc_recv.at[src], r, c).wait_recv()
+    for h in range(PARTS):
+        for k in range(1, C):
+            slices_wait(k, h)
+    own.wait()
+    for k in range(1, R):
+        tell_row(k).wait_send()
+    for k in range(1, C):
+        tell_col(k).wait_send()
+    for h in range(PARTS):
+        for k in range(1, C):
+            slices(k, h).wait_send()
+
+
+def begin(R, C, tiles, row_map, col_map, told):
+    hbm = pl.BlockSpec(memory_space=pltpu.HBM)
+    vmem = pl.BlockSpec(memory_space=pltpu.VMEM)
+    dma = pltpu.SemaphoreType.DMA
+    T, sub = tiles.shape[0], EDGE // C
     return pl.pallas_call(
-        functools.partial(place_kernel, C),
-        grid=(count // GROUP,),
-        in_specs=[pl.BlockSpec((GROUP, EDGE, EDGE), lambda t: (t, 0, 0)), whole, whole],
-        out_specs=pl.BlockSpec((C, GROUP, EDGE // C, EDGE), lambda t: (0, t, 0, 0)),
-        out_shape=jax.ShapeDtypeStruct((C, count, EDGE // C, EDGE), F32),
-        name="place",
-    )(tiles, row_map, col_map)
+        functools.partial(begin_kernel, R, C),
+        in_specs=[hbm, vmem, vmem, hbm],
+        out_specs=[hbm, hbm],
+        out_shape=[
+            jax.ShapeDtypeStruct((C * T, sub, EDGE), F32),
+            jax.ShapeDtypeStruct((C, R, 1, EDGE), jnp.int32),
+        ],
+        scratch_shapes=[
+            pltpu.VMEM((T, EDGE, EDGE), F32),
+            pltpu.VMEM((C, T, sub, EDGE), F32),
+            pltpu.VMEM((R, 1, EDGE), jnp.int32),
+            dma, dma((R,)), dma((R,)), dma((C,)), dma((C,)), dma((C, PARTS)), dma((C, PARTS)),
+        ],
+        compiler_params=pltpu.CompilerParams(
+            collective_id=4, has_side_effects=True, vmem_limit_bytes=60 << 20
+        ),
+        name="begin",
+    )(tiles, row_map, col_map, told)
 
 
 STEP = 8
@@ -111,20 +196,18 @@
     lax.fori_loop(0, EDGE // STEP, block, 0)
 
 
-PARTS = 4
 PACK = 4
 
 
 def spread_kernel(
-    R, C, cap2, cap3, placed, index2, index3, pick, col, grid, out, low_out,
+    R, C, cap2, cap3, parts3, held, index2, index3, pick, col, grid, out, low_out,
     r1, s2, r2, s3, stage, diag, mine, parts, work, upper, low,
     dr_send, dr_recv, dx_send, dx_recv, dy_send, dy_recv, m_send, m_recv, g_send, g_recv, low_sem,
-    st_in, st_out, b_send, b_recv, p1_send, p1_recv, p2_send, p2_recv, p3_send, p3_recv,
+    st_in, st_out, b_send, b_recv, load_sem, p2_send, p2_recv, p3_send, p3_recv,
 ):
     r = lax.axis_index("row")
     c = lax.axis_index("col")
     NB = R * C
-    T = placed.shape[1]
     start_of = lambda column: jnp.where(column < 2, 0, column)
     i0 = start_of(r * C + c)
     X = math.isqrt(C)
@@ -159,27 +242,8 @@
                 diag_row(p, k).start()
             diag_own(p).start()
 
-    part1 = T // PARTS
-
-    def first(k, h):
-        to = lax.rem(c + k, C)
-        return remote(
-            placed.at[to, pl.ds(h * part1, part1)], r1.at[pl.ds(c * T + h * part1, part1)],
-            p1_send.at[k, h], p1_recv.at[c, h], r, to,
-        )
-
-    def first_wait(k, h):
-        src = lax.rem(c + k, C)
-        remote(
-            placed.at[0, pl.ds(0, part1)], r1.at[pl.ds(src * T + h * part1, part1)],
-            p1_send.at[0, h], p1_recv.at[src, h], r, c,
-        ).wait_recv()
-
-    first_own = pltpu.make_async_copy(placed.at[c], r1.at[pl.ds(c * T, T)], p1_recv.at[c, 0])
-    first_own.start()
-    for h in range(PARTS):
-        for k in range(1, C):
-            first(k, h).start()
+    load = pltpu.make_async_copy(held, r1, load_sem)
+    load.start()
 
     def b_copy(i):
         return remote(
@@ -208,9 +272,7 @@
 
         over(low, high, run)
 
-    middle = i0 + (NB - i0) // 3
     own_blocks(lambda jl: own_in(jl).start())
-    sent_blocks(i0, middle, lambda i: b_copy(i).start())
 
     def own_turn(jl):
         own_in(jl).wait()
@@ -218,10 +280,7 @@
 
     own_blocks(own_turn)
 
-    first_own.wait()
-    for h in range(PARTS):
-        for k in range(1, C):
-            first_wait(k, h)
+    load.wait()
 
     for p in range(2):
 
@@ -321,10 +380,10 @@
     for k in range(1, C):
         mine_col(k).start()
     parts[c] = mine[...]
-    sent_blocks(middle, NB, lambda i: b_copy(i).start())
-
-
-    part3 = cap3 // PARTS
+    sent_blocks(i0, NB, lambda i: b_copy(i).start())
+
+
+    part3 = PACK * 4
 
     def third(k, h):
         to = lax.rem(c + k, C)
@@ -336,7 +395,8 @@
         at = pl.ds(h * part3, part3)
         remote(s3.at[0, at], out.at[src, at], p3_send.at[0, h], p3_recv.at[src, h], r, c).wait_recv()
 
-    third_own = pltpu.make_async_copy(s3.at[c], out.at[c], p3_recv.at[c, 0])
+    kept = pl.ds(0, parts3 * part3)
+    third_own = pltpu.make_async_copy(s3.at[c, kept], out.at[c, kept], p3_recv.at[c, 0])
 
     def pack3(k, h):
         to = lax.rem(c + k, C)
@@ -360,7 +420,7 @@
         pack3(C, h)
         third(C - 1, h).start()
 
-    over(0, PARTS, third_part)
+    over(0, parts3, third_part)
 
     @pl.when(y != 0)
     def _():
@@ -420,12 +480,9 @@
         over(0, C, run)
     third_own.start()
     sent_blocks(i0, NB, lambda i: b_copy(i).wait_send())
-    for h in range(PARTS):
-        for k in range(1, C):
-            first(k, h).wait_send()
     for k in range(1, R):
         second(k).wait_send()
-    for h in range(PARTS):
+    for h in range(parts3):
         for k in range(1, C):
             third_wait(k, h)
         for k in range(1, C):
@@ -448,13 +505,13 @@
         mine_col(k).wait_send()
 
 
-def spread(R, C, cap2, cap3, placed, index2, index3, pick, front):
+def spread(R, C, cap2, cap3, parts3, name, held, index2, index3, pick, front):
     hbm = pl.BlockSpec(memory_space=pltpu.HBM)
     smem = pl.BlockSpec(memory_space=pltpu.SMEM)
     dma = pltpu.SemaphoreType.DMA
-    T, sub = placed.shape[1], placed.shape[2]
+    sub = held.shape[1]
     return pl.pallas_call(
-        functools.partial(spread_kernel, R, C, cap2, cap3),
+        functools.partial(spread_kernel, R, C, cap2, cap3, parts3),
         in_specs=[hbm, smem, smem, smem, hbm],
         out_specs=[hbm, hbm, hbm],
         out_shape=[
@@ -463,7 +520,7 @@
             jax.ShapeDtypeStruct((5, EDGE, EDGE), F32),
         ],
         scratch_shapes=[
-            pltpu.VMEM((C * T, sub, EDGE), F32),
+            pltpu.VMEM(held.shape, F32),
             pltpu.VMEM((R, cap2, sub, EDGE), F32),
             pltpu.VMEM((R * cap2, sub, EDGE), F32),
             pltpu.VMEM((C, cap3, sub, EDGE), F32),
@@ -477,13 +534,13 @@
             dma((R,)), dma((2,)), dma((C,)), dma((2,)), dma((C,)), dma((1,)),
             dma((R,)), dma((2,)), dma((C,)), dma((C,)), dma,
             dma((C,)), dma((C,)), dma((R * C,)), dma((C, R)),
-            dma((C, PARTS)), dma((C, PARTS)), dma((R,)), dma((R,)), dma((C, PARTS)), dma((C, PARTS)),
+            dma, dma((R,)), dma((R,)), dma((C, parts3)), dma((C, parts3)),
         ],
         compiler_params=pltpu.CompilerParams(
-            collective_id=0, has_side_effects=True, vmem_limit_bytes=60 << 20
+            collective_id=name, has_side_effects=True, vmem_limit_bytes=60 << 20
         ),
         name="spread",
-    )(placed, index2, index3, pick, front)
+    )(held, index2, index3, pick, front)
 
 
 def slab_kernel(C, landing, grid, arrived, out, tile, sem):
@@ -785,8 +842,8 @@
 
 def capacities(R, C, T):
     if T < 32:
-        return 8, 16
-    return 104, 112
+        return 16, (PACK * 4, PACK * 8)
+    return 104, (80, 96, 128)
 
 
 def hot(values, count):
@@ -805,15 +862,16 @@
     C = lax.axis_size("col")
     count = R * C
     T = child_updates.shape[0]
-    cap2, cap3 = capacities(R, C, T)
+    cap2, choices = capacities(R, C, T)
+    cap3 = choices[-1]
     my_row = lax.axis_index("row").astype(jnp.int32)
     my_col = lax.axis_index("col").astype(jnp.int32)
 
     told = jnp.concatenate([target_columns[:, 0], row_offsets[:, 0]])
-    told = lax.all_to_all(
-        jnp.broadcast_to(told, (count, 2 * T)), ("row", "col"), split_axis=0, concat_axis=0, tiled=True
-    )
-    columns, offsets = told[:, :T], told[:, T:]
+    told = jnp.pad(told, (0, EDGE - 2 * T)).reshape(1, EDGE)
+    held, told = begin(R, C, child_updates, row_maps, col_maps, told)
+    told = told.reshape(C, R, EDGE).transpose(1, 0, 2).reshape(count, EDGE)
+    columns, offsets = told[:, :T], told[:, T : 2 * T]
     target_rows = columns + offsets % (count - columns)
     columns = columns.reshape(R, C * T)
     target_rows = target_rows.reshape(R, C * T)
@@ -836,7 +894,8 @@
     loads2 = jnp.sum(row_hot.astype(F32), axis=1)
     loads3 = jnp.einsum("pqk,pql->kl", row_hot, hot(to_col, C), preferred_element_type=F32)
     passes2 = (jnp.max(loads2).astype(jnp.int32) + cap2 - 1) // cap2
-    passes3 = (jnp.max(loads3).astype(jnp.int32) + cap3 - 1) // cap3
+    most3 = jnp.max(loads3).astype(jnp.int32)
+    passes3 = (most3 + cap3 - 1) // cap3
 
     def tables(a, b):
         own_hot = lax.dynamic_index_in_dim(row_hot, my_row, 0, keepdims=False)
@@ -865,21 +924,23 @@
     index2, index3, land_row, land_col, valid = tables(0, 0)
     marks = jnp.stack([mine & pivotal & (columns == k) & (rank2 < cap2) for k in range(2)])
     pick = jnp.einsum("vpq,pqn->vpn", marks.astype(BF16), hot(rank2, cap2), preferred_element_type=F32)
-    placed = place_tiles(C, child_updates, row_maps, col_maps)
-    grid, arrived, low = spread(
-        R, C, cap2, cap3, placed, index2, index3, pick.reshape(-1), front_entries.reshape(count, EDGE, EDGE)
+    runs = [
+        functools.partial(spread, R, C, cap2, cap3, size // (PACK * 4), 10 + at)
+        for at, size in enumerate(choices)
+    ]
+    choice = sum((most3 > size).astype(jnp.int32) for size in choices[:-1])
+    grid, arrived, low = lax.switch(
+        choice, runs, held, index2, index3, pick.reshape(-1), front_entries.reshape(count, EDGE, EDGE)
     )
 
     def another(carry):
         p, grid = carry
-        p, tiles = lax.optimization_barrier((p, placed))
         index2, index3, land_row, land_col, valid = tables(p // passes3, p % passes3)
-        held = lax.all_to_all(tiles, "col", split_axis=0, concat_axis=0, tiled=True)
-        held = held.reshape((C * T, EDGE // C, EDGE))[index2].reshape(R, cap2, EDGE // C, EDGE)
-        held = lax.all_to_all(held, "row", split_axis=0, concat_axis=0, tiled=True)
-        held = held.reshape((R * cap2, EDGE // C, EDGE))[index3].reshape(C, cap3, EDGE // C, EDGE)
-        held = lax.all_to_all(held, "col", split_axis=0, concat_axis=0, tiled=True)
-        tiles = held.transpose(1, 0, 2, 3).reshape(cap3, EDGE, EDGE)
+        moved = held[index2].reshape(R, cap2, EDGE // C, EDGE)
+        moved = lax.all_to_all(moved, "row", split_axis=0, concat_axis=0, tiled=True)
+        moved = moved.reshape((R * cap2, EDGE // C, EDGE))[index3].reshape(C, cap3, EDGE // C, EDGE)
+        moved = lax.all_to_all(moved, "col", split_axis=0, concat_axis=0, tiled=True)
+        tiles = moved.transpose(1, 0, 2, 3).reshape(cap3, EDGE, EDGE)
         tiles = jnp.where((valid > 0)[:, None, None], tiles, 0.0)
         return p + 1, grid.at[land_row, land_col].add(tiles)
 

time: 300 us -> 294 us (0.980)
  starting transfers between devices: 10.4 us -> 0 us
  Pallas kernels: 276 us -> 281 us
    pallas_call x2, Pallas kernels: 181 us -> 197 us  [the longest x1 159 us: spread(): pl.pallas_call(functools.partial(spread_kernel, R, C, cap2, cap3, parts3)...]
    pallas_call x1, Pallas kernels: 74.6 us -> 63.4 us  [panels(): pl.pallas_call(functools.partial(panel_kernel, R, C), in_specs=[hbm, pl.B...]
    all_to_all x1 -> x0, starting transfers between devices: 10.4 us -> none  [local(): lax.all_to_all(jnp.broadcast_to(told, (count, 2 * T)), ('row', 'col'), sp...]
  transfers between devices with their start and end apart: 1 -> 0, of which waited for: 0 -> 0; matrix products, arithmetic and copies ran while one was open for 0% -> 0% of each run, Pallas kernels for 3% -> 0%
where the time goes in v5:
time: 294 us; the launch traced here: 293 us
  Pallas kernels  281 us (96%)
  other arithmetic  4.53 us (2%)
  matrix products  2.98 us (1%)
    pallas_call x1, Pallas kernels, spread(): pl.pallas_call(functools.partial(spread_kernel, R, C, cap2, cap3, parts3)...  159 us
    pallas_call x1, Pallas kernels, panels(): pl.pallas_call(functools.partial(panel_kernel, R, C), in_specs=[hbm, pl.B...  63.4 us
    pallas_call x1, Pallas kernels, begin(): pl.pallas_call(functools.partial(begin_kernel, R, C), in_specs=[hbm, vmem...  37.7 us
    pallas_call x1, Pallas kernels, update(): pl.pallas_call(functools.partial(update_kernel, R, C), grid_spec=pltpu.Pr...  18.7 us

profile of v5, /device:TPU:12, one launch (start us, length us, event | category | flops | bytes accessed | tf_op | source)
XLA Modules:
  0.0 292.6 jit_solution(1744870588053795158)
XLA Ops:
  0.0 0.7 pad_add_fusion.3
  0.7 0.5 pad_bitcast_fusion.told
  1.3 0.7 pad_add_fusion.2.place
  2.0 37.7 %begin.1 = (f32[512,8,128]{2,1,0:T(8,128)S(1)}, s32[16,8,1,128]{3,2,1,0:T(1,128)}) custom-call(f32[32,128,128]{2,1,0:T(8,128)} %tiles.1, s32[32,128]{1,0:T(8,128)} %row_map.1, s32[32,128]{1,0:T(8,128)} %col_map.1, s32[1,128]{1,0:T(1,128)} %pad_bitcast_fusion.told), custom_call_target="tpu_custom_call" | custom-call | tf_op jit(solution)/shard_map/begin/pallas_call | solution.py:152
  39.7 0.9 copy.76
  40.6 0.8 fusion.110
  41.3 0.1 reshape.1008
  41.4 0.1 reshape.1010
  41.5 0.1 reshape.1009
  41.6 0.1 reshape.1011
  41.7 0.1 convert_reduce_fusion.2
  41.8 0.6 reduce_max.19
  43.1 0.3 fusion.47
  43.4 0.3 fusion.48
  43.8 0.2 convolution_convert_fusion.1
  43.9 0.1 add.354
  44.0 0.4 fusion.55
  44.4 0.1 reshape.1012
  44.5 0.8 fusion.63
  46.0 0.1 convert_reduce_fusion
  46.1 0.1 select_reduce_fusion
  46.2 0.3 fusion.43
  46.5 0.6 fusion.111
  47.2 0.8 fusion.52
  48.0 0.6 pad_add_fusion.1.landing
  48.6 159.5 %conditional.1 = ((f32[16,8,128,128]{3,2,1,0:T(8,128)}, f32[16,128,8,128]{3,2,1,0:T(8,128)}, f32[5,128,128]{2,1,0:T(8,128)})) conditional(s32[]{:T(128)} %clamp.3, (f32[512,8,128]{2,1,0:T(8,128)S(1)}, s32[832]{0:T(1024)S(1)}, s32[2048]{0:T(1024)S(1)}, f32[1664]{0:T(1024)S(1)}, f32[128,128,128]{2,1,0:T(8,128)}) %tuple.70, ...), branch_computations={%region_6.7_spmd, %region_7.8_spmd, %region_8.9_spmd} | conditional | bytes 8 | solution.py:932
  48.6 159.3 %spread.5 = (f32[16,8,128,128]{3,2,1,0:T(8,128)}, f32[16,128,8,128]{3,2,1,0:T(8,128)}, f32[5,128,128]{2,1,0:T(8,128)}) custom-call(f32[512,8,128]{2,1,0:T(8,128)S(1)} %get-tuple-element.352.held, s32[832]{0:T(1024)S(1)} %get-tuple-element.353.index2, s32[2048]{0:T(1024)S(1)} %get-tuple-element.354.index3, f32[1664]{0:T(1024)S(1)} %get-tuple-element.355.pick, ...), custom_call_target="tpu_custom_call" | custom-call | tf_op jit(solution)/shard_map/cond/branch_2_fun/spread/pallas_call | solution.py:513
  208.2 0.0 copy-start.2
  208.2 2.3 slab.1
  210.5 0.0 copy-done.2
  210.5 63.4 %panels.1 = (f32[2,16,128,128]{3,2,1,0:T(8,128)}, f32[2,8,128,128]{3,2,1,0:T(8,128)}) custom-call(f32[16,128,128]{2,1,0:T(8,128)} %slab.1, f32[5,128,128]{2,1,0:T(8,128)S(1)} %copy-done.2), custom_call_target="tpu_custom_call" | custom-call | tf_op jit(solution)/shard_map/panels/pallas_call | solution.py:712
  273.9 18.7 %update.1 = f32[16,8,128,128]{3,2,1,0:T(8,128)} custom-call(s32[2]{0:T(128)} %pad_add_fusion.2.place, s32[257]{0:T(512)} %pad_add_fusion.1.landing, f32[16,8,128,128]{3,2,1,0:T(8,128)} %get-tuple-element.393.grid, f32[2,16,128,128]{3,2,1,0:T(8,128)} %get-tuple-element.396.qrow, f32[2,8,128,128]{3,2,1,0:T(8,128)} %get-tuple-element.397.qcol, ...), custom_call_target="tpu_custom_call" | custom-call | tf_op jit(solution)/shard_map/update/pallas_call | solution.py:818
  (27 shorter events, 0.3 us)
Async XLA Ops:
  208.2 2.4 copy-start.2

commit v6 on v5

--- a/solution.py
+++ b/solution.py
@@ -54,9 +54,9 @@
 
 
 def begin_kernel(
-    R, C, tiles, row_map, col_map, told, r1, told_all,
-    held, placed, told_row,
-    t_sem, tr_send, tr_recv, tc_send, tc_recv, send, recv,
+    R, C, tiles, row_map, col_map, told, col, r1, told_all, slab,
+    held, placed, told_row, stage,
+    st_in, st_out, f_send, f_recv, t_sem, tr_send, tr_recv, tc_send, tc_recv, send, recv,
 ):
     r = lax.axis_index("row")
     c = lax.axis_index("col")
@@ -77,6 +77,30 @@
     tell_own.start()
     for k in range(1, R):
         tell_row(k).start()
+
+    def ahead(i):
+        return remote(col.at[i], slab.at[i // R], f_send.at[i], f_recv.at[i // R], lax.rem(i, R), c)
+
+    def others(body):
+        def run(i):
+            @pl.when(lax.rem(i, R) != 0)
+            def _():
+                body(i)
+
+        over(0, R * C, run)
+
+    def own_in(jl):
+        return pltpu.make_async_copy(col.at[jl * R], stage.at[jl], st_in.at[jl])
+
+    def own_out(jl):
+        return pltpu.make_async_copy(stage.at[jl], slab.at[jl], st_out.at[jl])
+
+    panel = (r == 0) & (c < 2)
+
+    @pl.when(panel)
+    def _():
+        over(0, C, lambda jl: own_in(jl).start())
+        others(lambda i: ahead(i).start())
 
     levels = lax.broadcasted_iota(jnp.int32, (EDGE, EDGE), 0)
 
@@ -127,6 +151,24 @@
             slices(k, h).start()
     own = pltpu.make_async_copy(placed.at[c], r1.at[pl.ds(c * T, T)], recv.at[c, 0])
     own.start()
+
+    @pl.when(panel)
+    def _():
+        def turn(jl):
+            own_in(jl).wait()
+            own_out(jl).start()
+
+        over(0, C, turn)
+        over(0, C, lambda jl: own_out(jl).wait())
+        others(lambda i: ahead(i).wait_send())
+
+    @pl.when((r != 0) & (c < 2))
+    def _():
+        def landed(jl):
+            remote(col.at[0], slab.at[jl], f_send.at[0], f_recv.at[jl], r, c).wait_recv()
+
+        over(0, C, landed)
+
     tell_kept.wait()
     for k in range(1, C):
         src = lax.rem(c + k, C)
@@ -144,30 +186,33 @@
             slices(k, h).wait_send()
 
 
-def begin(R, C, tiles, row_map, col_map, told):
+def begin(R, C, tiles, row_map, col_map, told, front):
     hbm = pl.BlockSpec(memory_space=pltpu.HBM)
     vmem = pl.BlockSpec(memory_space=pltpu.VMEM)
     dma = pltpu.SemaphoreType.DMA
     T, sub = tiles.shape[0], EDGE // C
     return pl.pallas_call(
         functools.partial(begin_kernel, R, C),
-        in_specs=[hbm, vmem, vmem, hbm],
-        out_specs=[hbm, hbm],
+        in_specs=[hbm, vmem, vmem, hbm, hbm],
+        out_specs=[hbm, hbm, hbm],
         out_shape=[
             jax.ShapeDtypeStruct((C * T, sub, EDGE), F32),
             jax.ShapeDtypeStruct((C, R, 1, EDGE), jnp.int32),
+            jax.ShapeDtypeStruct((C, EDGE, EDGE), F32),
         ],
         scratch_shapes=[
             pltpu.VMEM((T, EDGE, EDGE), F32),
             pltpu.VMEM((C, T, sub, EDGE), F32),
             pltpu.VMEM((R, 1, EDGE), jnp.int32),
+            pltpu.VMEM((C, EDGE, EDGE), F32),
+            dma((C,)), dma((C,)), dma((R * C,)), dma((C,)),
             dma, dma((R,)), dma((R,)), dma((C,)), dma((C,)), dma((C, PARTS)), dma((C, PARTS)),
         ],
         compiler_params=pltpu.CompilerParams(
             collective_id=4, has_side_effects=True, vmem_limit_bytes=60 << 20
         ),
         name="begin",
-    )(tiles, row_map, col_map, told)
+    )(tiles, row_map, col_map, told, front)
 
 
 STEP = 8
@@ -200,15 +245,15 @@
 
 
 def spread_kernel(
-    R, C, cap2, cap3, parts3, held, index2, index3, pick, col, grid, out, low_out,
-    r1, s2, r2, s3, stage, diag, mine, parts, work, upper, low,
+    R, C, cap2, cap3, parts3, held, index2, index3, pick, chosen, slab, col, grid, out, low_out, chunk_out,
+    r1, s2, r2, s3, stage, chunk, sums, child, c_send, ck_recv, ch_send, ch_recv, chunk_sem, diag, mine, parts, work, upper, low,
     dr_send, dr_recv, dx_send, dx_recv, dy_send, dy_recv, m_send, m_recv, g_send, g_recv, low_sem,
     st_in, st_out, b_send, b_recv, load_sem, p2_send, p2_recv, p3_send, p3_recv,
 ):
     r = lax.axis_index("row")
     c = lax.axis_index("col")
     NB = R * C
-    start_of = lambda column: jnp.where(column < 2, 0, column)
+    start_of = lambda column: jnp.where(column < 2, NB, column)
     i0 = start_of(r * C + c)
     X = math.isqrt(C)
     x, y = lax.rem(c, X), c // X
@@ -318,6 +363,22 @@
 
     over(0, cap2 // PACK, pack2_own)
     second(R - 1).start()
+
+    def scatter(jl, k):
+        return remote(slab.at[jl], chunk.at[k], c_send.at[jl], ck_recv.at[k], r, jl)
+
+    def scatter_own(jl, k):
+        return pltpu.make_async_copy(slab.at[jl], chunk.at[k], ck_recv.at[k])
+
+    for k in range(2):
+
+        @pl.when(c == k)
+        def _():
+            for jl in range(C):
+                if jl == k:
+                    scatter_own(jl, k).start()
+                else:
+                    scatter(jl, k).start()
 
     @pl.when(y == 0)
     def _():
@@ -422,6 +483,28 @@
 
     over(0, parts3, third_part)
 
+    def send_sums(k):
+        to = lax.rem(c + k, C)
+        return remote(sums.at[pl.ds(2 * to, 2)], child.at[c], ch_send.at[k], ch_recv.at[c], r, to)
+
+    sums[...] = jnp.zeros(sums.shape, F32)
+
+    def add_up(p):
+        for u in range(sums.shape[1]):
+            rest = r2[pl.ds(p * cap2, cap2), u, :]
+            total = sums[:, u, :]
+            for _ in range(3):
+                piece = rest.astype(BF16)
+                rest = rest - piece.astype(F32)
+                total = total + dot16(chosen[p], piece, NN)
+            sums[:, u, :] = total
+
+    over(0, R, add_up)
+    for k in range(1, C):
+        send_sums(k).start()
+    for b in range(2):
+        child[c, b] = sums[2 * c + b]
+
     @pl.when(y != 0)
     def _():
         remote(diag, diag, dy_send.at[0], dy_recv.at[0], r, c).wait_recv()
@@ -467,6 +550,22 @@
     pivot(diag[2] - dot(low[2], low[2], NT), 3)
     low_copy = pltpu.make_async_copy(low, low_out, low_sem)
     low_copy.start()
+
+    scatter_own(0, 0).wait()
+    scatter_own(0, 1).wait()
+
+    def child_wait(q):
+        @pl.when(q != c)
+        def _():
+            remote(sums.at[pl.ds(0, 2)], child.at[q], ch_send.at[0], ch_recv.at[q], r, c).wait_recv()
+
+    over(0, C, child_wait)
+    for q in range(C):
+        for b in range(2):
+            at = pl.ds(q * sub, sub)
+            chunk[b, at, :] = chunk[b, at, :] + child[q, b]
+    chunk_copy = pltpu.make_async_copy(chunk, chunk_out, chunk_sem)
+    chunk_copy.start()
 
     own_blocks(lambda jl: own_out(jl).wait())
     for s in range(R):
@@ -489,6 +588,17 @@
             third(k, h).wait_send()
     third_own.wait()
     low_copy.wait()
+    chunk_copy.wait()
+    for k in range(1, C):
+        send_sums(k).wait_send()
+    for k in range(2):
+
+        @pl.when(c == k)
+        def _():
+            for jl in range(C):
+                if jl != k:
+                    scatter(jl, k).wait_send()
+
     for p in range(2):
 
         @pl.when((r == 0) & (c == pieces[p][0]))
@@ -505,19 +615,20 @@
         mine_col(k).wait_send()
 
 
-def spread(R, C, cap2, cap3, parts3, name, held, index2, index3, pick, front):
+def spread(R, C, cap2, cap3, parts3, name, held, index2, index3, pick, chosen, slab, front):
     hbm = pl.BlockSpec(memory_space=pltpu.HBM)
     smem = pl.BlockSpec(memory_space=pltpu.SMEM)
     dma = pltpu.SemaphoreType.DMA
     sub = held.shape[1]
     return pl.pallas_call(
         functools.partial(spread_kernel, R, C, cap2, cap3, parts3),
-        in_specs=[hbm, smem, smem, smem, hbm],
-        out_specs=[hbm, hbm, hbm],
+        in_specs=[hbm, smem, smem, smem, pl.BlockSpec(memory_space=pltpu.VMEM), hbm, hbm],
+        out_specs=[hbm, hbm, hbm, hbm],
         out_shape=[
             jax.ShapeDtypeStruct((C, R, EDGE, EDGE), F32),
             jax.ShapeDtypeStruct((C, cap3, sub, EDGE), F32),
             jax.ShapeDtypeStruct((5, EDGE, EDGE), F32),
+            jax.ShapeDtypeStruct((2, EDGE, EDGE), F32),
         ],
         scratch_shapes=[
             pltpu.VMEM(held.shape, F32),
@@ -525,6 +636,10 @@
             pltpu.VMEM((R * cap2, sub, EDGE), F32),
             pltpu.VMEM((C, cap3, sub, EDGE), F32),
             pltpu.VMEM((C, EDGE, EDGE), F32),
+            pltpu.VMEM((2, EDGE, EDGE), F32),
+            pltpu.VMEM((2 * C, sub, EDGE), F32),
+            pltpu.VMEM((C, 2, sub, EDGE), F32),
+            dma((C,)), dma((2,)), dma((C,)), dma((C,)), dma,
             pltpu.VMEM((3, EDGE, EDGE), F32),
             pltpu.VMEM((3, sub, EDGE), F32),
             pltpu.VMEM((C, 3, sub, EDGE), F32),
@@ -540,74 +655,21 @@
             collective_id=name, has_side_effects=True, vmem_limit_bytes=60 << 20
         ),
         name="spread",
-    )(held, index2, index3, pick, front)
-
-
-def slab_kernel(C, landing, grid, arrived, out, tile, sem):
-    out[...] = grid[:, 0]
-    slots = arrived.shape[1]
-
-    def run(k):
-        @pl.when(landing[1 + slots + k] == 0)
-        def _():
-            copy = pltpu.make_async_copy(arrived.at[:, k], tile, sem)
-            copy.start()
-            copy.wait()
-            jl = landing[1 + k]
-            out[jl] = out[jl] + tile[...].reshape(EDGE, EDGE)
-
-    @pl.when(landing[0] < 2)
-    def _():
-        over(0, slots, run)
-
-
-def slab_of(C, landing, grid, arrived):
-    return pl.pallas_call(
-        functools.partial(slab_kernel, C),
-        grid=(1,),
-        in_specs=[
-            pl.BlockSpec(memory_space=pltpu.SMEM),
-            pl.BlockSpec((C, 1, EDGE, EDGE), lambda t: (0, 0, 0, 0)),
-            pl.BlockSpec(memory_space=pltpu.HBM),
-        ],
-        out_specs=pl.BlockSpec((C, EDGE, EDGE), lambda t: (0, 0, 0)),
-        out_shape=jax.ShapeDtypeStruct((C, EDGE, EDGE), F32),
-        scratch_shapes=[pltpu.VMEM((arrived.shape[0], EDGE // C, EDGE), F32), pltpu.SemaphoreType.DMA],
-        compiler_params=pltpu.CompilerParams(vmem_limit_bytes=60 << 20),
-        name="slab",
-    )(landing, grid, arrived)
+    )(held, index2, index3, pick, chosen, slab, front)
 
 
 def panel_kernel(
-    R, C, slab, low, qrow, qcol,
-    chunk, rows_q, zbuf, cols_q,
-    sc_send, ck_recv, ag_send, ag_recv, z_send, z_recv, v_send, v_recv, q_sem,
+    R, C, chunk, low, qrow, qcol,
+    rows_q, zbuf, cols_q,
+    ag_send, ag_recv, z_send, z_recv, v_send, v_recv, q_sem,
 ):
     r = lax.axis_index("row")
     c = lax.axis_index("col")
     ratio = C // R
     greet(R, C, r, c)
 
-    def scatter(jl, k):
-        return remote(slab.at[jl], chunk.at[k], sc_send.at[jl], ck_recv.at[k], r, jl)
-
-    def scatter_own(jl, k):
-        return pltpu.make_async_copy(slab.at[jl], chunk.at[k], ck_recv.at[k])
-
-    for k in range(2):
-
-        @pl.when(c == k)
-        def _():
-            for jl in range(C):
-                if jl == k:
-                    scatter_own(jl, k).start()
-                else:
-                    scatter(jl, k).start()
-
     i = c * R + r
-    scatter_own(0, 0).wait()
     q0 = dot(chunk[0], low[1], NT)
-    scatter_own(0, 1).wait()
     q1 = dot(chunk[1] - dot(q0, low[2], NT), low[4], NT)
     rows_q[0, c] = jnp.where(i == 0, low[0], jnp.where(i == 1, low[2], q0))
     rows_q[1, c] = jnp.where(i == 0, 0.0, jnp.where(i == 1, low[3], q1))
@@ -681,14 +743,6 @@
     keep_col = pltpu.make_async_copy(cols_q, qcol, q_sem.at[0])
     keep_col.start()
 
-    for k in range(2):
-
-        @pl.when(c == k)
-        def _():
-            for jl in range(C):
-                if jl != k:
-                    scatter(jl, k).wait_send()
-
     for n in range(2):
         for k in range(1, C):
             gather(k, n).wait_send()
@@ -706,30 +760,29 @@
     keep_row.wait()
 
 
-def panels(R, C, slab, low):
+def panels(R, C, chunk, low):
     hbm = pl.BlockSpec(memory_space=pltpu.HBM)
     dma = pltpu.SemaphoreType.DMA
     return pl.pallas_call(
         functools.partial(panel_kernel, R, C),
-        in_specs=[hbm, pl.BlockSpec(memory_space=pltpu.VMEM)],
+        in_specs=[pl.BlockSpec(memory_space=pltpu.VMEM)] * 2,
         out_specs=[hbm, hbm],
         out_shape=[
             jax.ShapeDtypeStruct((2, C, EDGE, EDGE), F32),
             jax.ShapeDtypeStruct((2, R, EDGE, EDGE), F32),
         ],
         scratch_shapes=[
-            pltpu.VMEM((2, EDGE, EDGE), F32),
             pltpu.VMEM((2, C, EDGE, EDGE), F32),
             pltpu.VMEM((2, R, EDGE, EDGE), F32),
             pltpu.VMEM((2, R, EDGE, EDGE), F32),
-            dma((C,)), dma((2,)), dma((2, C)), dma((2, C)),
+            dma((2, C)), dma((2, C)),
             dma((2, R)), dma((2, R)), dma((2, R)), dma((2, R)), dma((2,)),
         ],
         compiler_params=pltpu.CompilerParams(
             collective_id=1, has_side_effects=True, vmem_limit_bytes=60 << 20
         ),
         name="panels",
-    )(slab, low)
+    )(chunk, low)
 
 
 def halves(x):
@@ -737,9 +790,10 @@
     return high, (x - high.astype(F32)).astype(BF16)
 
 
-def update_kernel(R, C, place, landing, grid, qrow, qcol, arrived, out, left, right, head, follow):
+def update_kernel(R, C, place, landing, grid, qrow, qcol, source, out, arrived, left, right, head, follow, sem):
     s = pl.program_id(0)
     slots = arrived.shape[1]
+    batch = PACK * 4
     r, c = place[0], place[1]
     j = s * C + c
     rows = lax.broadcasted_iota(jnp.int32, (EDGE, EDGE), 0)
@@ -752,7 +806,7 @@
 
         over(0, R, clear)
 
-        def link(k):
+        def link(k, used):
             where = landing[1 + slots + k]
 
             @pl.when(where >= 0)
@@ -760,7 +814,16 @@
                 follow[k] = head[where]
                 head[where] = k
 
-        over(0, slots, link)
+            return jnp.where(where >= 0, k + 1, used)
+
+        used = lax.fori_loop(0, slots, link, 0)
+        batches = lax.div(used + batch - 1, batch)
+
+        def load(b):
+            at = pl.ds(pl.multiple_of(b * batch, batch), batch)
+            return pltpu.make_async_copy(source.at[:, at], arrived.at[:, at], sem.at[b])
+
+        over(0, batches, lambda b: load(b).start())
 
         def split(jl):
             at = pl.ds(pl.multiple_of(jl * EDGE, EDGE), EDGE)
@@ -770,6 +833,7 @@
                     left[at, (m + n) * EDGE : (m + n + 1) * EDGE] = part
 
         over(0, C, split)
+        over(0, batches, lambda b: load(b).wait())
 
     for n in range(2):
         high, low = halves(qcol[n, 0])
@@ -824,14 +888,16 @@
                 block,
                 pl.BlockSpec((2, C, EDGE, EDGE), lambda s, *_: (0, 0, 0, 0)),
                 pl.BlockSpec((2, 1, EDGE, EDGE), lambda s, *_: (0, s, 0, 0)),
-                pl.BlockSpec(arrived.shape, lambda s, *_: (0, 0, 0, 0), pipeline_mode=pl.Buffered(1)),
+                pl.BlockSpec(memory_space=pltpu.HBM),
             ],
             out_specs=block,
             scratch_shapes=[
+                pltpu.VMEM(arrived.shape, F32),
                 pltpu.VMEM((C * EDGE, 6 * EDGE), BF16),
                 pltpu.VMEM((6 * EDGE, EDGE), BF16),
                 pltpu.SMEM((R,), jnp.int32),
                 pltpu.SMEM((cap3,), jnp.int32),
+                pltpu.SemaphoreType.DMA((cap3 // (PACK * 4),)),
             ],
         ),
         out_shape=jax.ShapeDtypeStruct((C, R, EDGE, EDGE), F32),
@@ -843,7 +909,7 @@
 def capacities(R, C, T):
     if T < 32:
         return 16, (PACK * 4, PACK * 8)
-    return 104, (80, 96, 128)
+    return 104, (80, 112, 160)
 
 
 def hot(values, count):
@@ -869,7 +935,8 @@
 
     told = jnp.concatenate([target_columns[:, 0], row_offsets[:, 0]])
     told = jnp.pad(told, (0, EDGE - 2 * T)).reshape(1, EDGE)
-    held, told = begin(R, C, child_updates, row_maps, col_maps, told)
+    front = front_entries.reshape(count, EDGE, EDGE)
+    held, told, slab = begin(R, C, child_updates, row_maps, col_maps, told, front)
     told = told.reshape(C, R, EDGE).transpose(1, 0, 2).reshape(count, EDGE)
     columns, offsets = told[:, :T], told[:, T : 2 * T]
     target_rows = columns + offsets % (count - columns)
@@ -878,8 +945,8 @@
     to_row, to_col = target_rows % R, columns % C
 
     row_hot = hot(to_row, R)
-    pivotal = (target_rows < 2) & (columns < 2)
-    lead = row_hot * pivotal[..., None].astype(BF16)
+    panel = columns < 2
+    lead = row_hot * panel[..., None].astype(BF16)
     rest = row_hot - lead
     leads = jnp.sum(lead.astype(F32), axis=1, keepdims=True)
     rank2 = before(lead) * lead.astype(F32) + (before(rest) + leads) * rest.astype(F32)
@@ -922,15 +989,17 @@
         return index2, index3, here[2], here[3], here[4]
 
     index2, index3, land_row, land_col, valid = tables(0, 0)
-    marks = jnp.stack([mine & pivotal & (columns == k) & (rank2 < cap2) for k in range(2)])
-    pick = jnp.einsum("vpq,pqn->vpn", marks.astype(BF16), hot(rank2, cap2), preferred_element_type=F32)
+    marks = hot(jnp.where(mine & panel, target_rows // R * 2 + columns, -1), 2 * C)
+    chosen = jnp.einsum("pqv,pqn->pvn", marks, hot(rank2, cap2), preferred_element_type=F32)
+    pick = chosen[:, :2].transpose(1, 0, 2).reshape(-1)
+    chosen = chosen.astype(BF16)
     runs = [
         functools.partial(spread, R, C, cap2, cap3, size // (PACK * 4), 10 + at)
         for at, size in enumerate(choices)
     ]
     choice = sum((most3 > size).astype(jnp.int32) for size in choices[:-1])
-    grid, arrived, low = lax.switch(
-        choice, runs, held, index2, index3, pick.reshape(-1), front_entries.reshape(count, EDGE, EDGE)
+    grid, arrived, low, chunk = lax.switch(
+        choice, runs, held, index2, index3, pick, chosen, slab, front
     )
 
     def another(carry):
@@ -947,8 +1016,7 @@
     _, grid = lax.while_loop(lambda carry: carry[0] < passes2 * passes3, another, (jnp.int32(1), grid))
 
     landing = jnp.concatenate([my_col[None], land_row, jnp.where(valid > 0, land_col, -1)])
-    slab = slab_of(C, landing, grid, arrived)
-    qrow, qcol = panels(R, C, slab, low)
+    qrow, qcol = panels(R, C, chunk, low)
     place = jnp.stack([my_row, my_col])
     result = update(R, C, place, landing, grid, qrow, qcol, arrived)
     return result.reshape(C, 1, R, 1, EDGE, EDGE)

time: 294 us -> 280 us (0.952)
  the two profiles are of different devices: /device:TPU:12 before, /device:TPU:78 now
where the time goes in v6:
time: 280 us
  Pallas kernels  263 us (94%)
  other arithmetic  7.07 us (3%)
  matrix products  4.27 us (2%)
  local copies, waits for them, and re-layouts  3.79 us (1%)
    pallas_call x1, Pallas kernels, spread(): pl.pallas_call(functools.partial(spread_kernel, R, C, cap2, cap3, parts3)...  151 us
    pallas_call x1, Pallas kernels, panels(): pl.pallas_call(functools.partial(panel_kernel, R, C), in_specs=[pl.BlockS...  56.2 us
    pallas_call x1, Pallas kernels, begin(): pl.pallas_call(functools.partial(begin_kernel, R, C), in_specs=[hbm, vmem...  37.5 us
    pallas_call x1, Pallas kernels, update(): pl.pallas_call(functools.partial(update_kernel, R, C), grid_spec=pltpu.Pr...  17.6 us

profile of v6, /device:TPU:78, one launch (start us, length us, event | category | flops | bytes accessed | tf_op | source)
XLA Modules:
  0.0 279.7 jit_solution(18416782897607640022)
XLA Ops:
  0.0 0.7 pad_add_fusion.2
  0.7 0.5 pad_bitcast_fusion.told
  1.3 0.6 pad_add_fusion.1.place
  1.9 0.6 pad_maximum_fusion.1
  2.5 37.5 %begin.1 = (f32[512,8,128]{2,1,0:T(8,128)S(1)}, s32[16,8,1,128]{3,2,1,0:T(1,128)}, f32[16,128,128]{2,1,0:T(8,128)S(1)}) custom-call(f32[32,128,128]{2,1,0:T(8,128)} %tiles.1, s32[32,128]{1,0:T(8,128)} %row_map.1, s32[32,128]{1,0:T(8,128)} %col_map.1, s32[1,128]{1,0:T(1,128)} %pad_bitcast_fusion.told, f32[128,128,128]{2,1,0:T(8,128)} %bitcast.155), custom_call_target="tpu_custom_call" | custom-call | tf_op jit(solution)/shard_map/begin/pallas_call | solution.py:194
  40.0 0.9 copy.16
  40.8 0.8 fusion.74
  41.6 0.1 reshape.930
  41.7 0.7 reshape.932
  42.4 0.1 reshape.929
  42.5 0.7 reshape.931
  43.2 0.6 fusion.94
  43.8 0.1 convert_reduce_fusion.2
  43.9 0.6 reduce_max.19
  45.1 0.8 fusion.60
  46.5 0.1 convert_reduce_fusion
  46.6 0.1 select_reduce_fusion
  46.7 0.3 fusion.42
  47.0 0.6 constant_dynamic-slice_fusion.3
  47.7 0.3 fusion.46
  47.9 0.3 fusion.53
  48.3 0.8 convolution_convert_fusion.1
  49.2 0.7 fusion.108
  50.0 1.3 fusion.107
  51.3 0.7 fusion.50
  52.1 0.7 pad_add_fusion.landing
  52.7 1.2 fusion.109
  54.0 151.4 %conditional.1 = ((f32[16,8,128,128]{3,2,1,0:T(8,128)}, f32[16,160,8,128]{3,2,1,0:T(8,128)}, f32[5,128,128]{2,1,0:T(8,128)}, f32[2,128,128]{2,1,0:T(8,128)})) conditional(s32[]{:T(128)} %clamp.3, (f32[512,8,128]{2,1,0:T(8,128)S(1)}, s32[832]{0:T(1024)S(1)}, s32[2560]{0:T(1024)S(1)}, f32[1664]{0:T(1024)S(1)}, ...), branch_computations={%region_6.7_spmd, %region_7.8_spmd, %region_8.9_spmd} | conditional | bytes 8 | solution.py:1001
  54.0 151.2 %spread.3 = (f32[16,8,128,128]{3,2,1,0:T(8,128)}, f32[16,160,8,128]{3,2,1,0:T(8,128)}, f32[5,128,128]{2,1,0:T(8,128)}, f32[2,128,128]{2,1,0:T(8,128)}) custom-call(f32[512,8,128]{2,1,0:T(8,128)S(1)} %get-tuple-element.354.held, s32[832]{0:T(1024)S(1)} %get-tuple-element.355.index2, s32[2560]{0:T(1024)S(1)} %get-tuple-element.356.index3, ...), custom_call_target="tpu_custom_call" | custom-call | tf_op jit(solution)/shard_map/cond/branch_0_fun/spread/pallas_call | solution.py:623
  205.5 0.2 while.14
  205.7 56.2 %panels.1 = (f32[2,16,128,128]{3,2,1,0:T(8,128)}, f32[2,8,128,128]{3,2,1,0:T(8,128)}) custom-call(f32[2,128,128]{2,1,0:T(8,128)} %get-tuple-element.415.chunk, f32[5,128,128]{2,1,0:T(8,128)} %get-tuple-element.416.low), custom_call_target="tpu_custom_call" | custom-call | tf_op jit(solution)/shard_map/panels/pallas_call | solution.py:766
  261.9 17.6 %update.1 = f32[16,8,128,128]{3,2,1,0:T(8,128)} custom-call(s32[2]{0:T(128)} %pad_add_fusion.1.place, s32[321]{0:T(512)} %pad_add_fusion.landing, f32[16,8,128,128]{3,2,1,0:T(8,128)} %get-tuple-element.784, f32[2,16,128,128]{3,2,1,0:T(8,128)} %get-tuple-element.417.qrow, f32[2,8,128,128]{3,2,1,0:T(8,128)} %get-tuple-element.418.qcol, ...), custom_call_target="tpu_custom_call" | custom-call | tf_op jit(solution)/shard_map/update/pallas_call | solution.py:882
  (25 shorter events, 0.4 us)
Async XLA Ops:
  54.0 151.4 %copy-start.7 = (bf16[1,512,8]{1,2,0:T(8,128)(2,1)S(1)}, bf16[1,512,8]{1,2,0:T(8,128)(2,1)}, u32[]{:S(2)}) copy-start(bf16[1,512,8]{1,2,0:T(8,128)(2,1)} %constant_dynamic-slice_fusion.3) | copy-start | bytes 24580
